TPU v7x, 32 devices: a whole 2x2x4 slice. The times are simulated.
32 devices in a mesh: head: 4 (over x, core), blk: 8 (over z, y).
Axes of the slice: x: 2, y: 2, z: 4, core: 2. Of those that a mesh axis runs over, the one named last changes fastest.
Arguments:
- tokens: bfloat16 [8, 1024, 768], P('head', 'blk'), may hold values from -6 to 6
- lengths: int32 [8], replicated, may hold values from 256 to 1024, as said below
- slot_sequence: int32 [8], replicated, may hold values from 0 to 7, each once
- cotangent: bfloat16 [8, 1024, 768], P('head', 'blk'), may hold values from -6 to 6
- w_query: bfloat16 [2, 768, 768], P(None, ('head', 'blk')), may hold values from -0.3125 to 0.3125
- w_key: bfloat16 [2, 768, 768], P(None, ('head', 'blk')), may hold values from -0.3125 to 0.3125
- w_value: bfloat16 [2, 768, 768], P(None, ('head', 'blk')), may hold values from -0.21875 to 0.21875
- w_out: bfloat16 [2, 768, 768], P(None, ('head', 'blk')), may hold values from -1.25 to 1.25
- w_in: bfloat16 [2, 768, 3072], P(None, ('head', 'blk')), may hold values from -0.21875 to 0.21875
- w_down: bfloat16 [2, 3072, 768], P(None, ('head', 'blk')), may hold values from -0.109375 to 0.109375
- b_query: bfloat16 [2, 768], P(None, ('head', 'blk')), may hold values from -3 to 3
- b_value: bfloat16 [2, 768], P(None, ('head', 'blk')), may hold values from -3 to 3
- b_out: bfloat16 [2, 768], P(None, ('head', 'blk')), may hold values from -3 to 3
- b_in: bfloat16 [2, 3072], P(None, ('head', 'blk')), may hold values from -3 to 3
- b_down: bfloat16 [2, 768], P(None, ('head', 'blk')), may hold values from -3 to 3
- norm1_gain: bfloat16 [2, 768], P(None, ('head', 'blk')), may hold values from 0.5 to 1.5
- norm1_bias: bfloat16 [2, 768], P(None, ('head', 'blk')), may hold values from -2 to 2
- norm2_gain: bfloat16 [2, 768], P(None, ('head', 'blk')), may hold values from 0.5 to 1.5
- norm2_bias: bfloat16 [2, 768], P(None, ('head', 'blk')), may hold values from -2 to 2
Outputs:
- block_out: float32 [8, 1024, 768], P('head', 'blk')
- grad_tokens: float32 [8, 1024, 768], P('head', 'blk')
- grad_w_query: float32 [2, 768, 768], P(None, ('head', 'blk'))
- grad_w_key: float32 [2, 768, 768], P(None, ('head', 'blk'))
- grad_w_value: float32 [2, 768, 768], P(None, ('head', 'blk'))
- grad_w_out: float32 [2, 768, 768], P(None, ('head', 'blk'))
- grad_w_in: float32 [2, 768, 3072], P(None, ('head', 'blk'))
- grad_w_down: float32 [2, 3072, 768], P(None, ('head', 'blk'))
- grad_b_query: float32 [2, 768], P(None, ('head', 'blk'))
- grad_b_value: float32 [2, 768], P(None, ('head', 'blk'))
- grad_b_out: float32 [2, 768], P(None, ('head', 'blk'))
- grad_b_in: float32 [2, 3072], P(None, ('head', 'blk'))
- grad_b_down: float32 [2, 768], P(None, ('head', 'blk'))
- grad_norm1_gain: float32 [2, 768], P(None, ('head', 'blk'))
- grad_norm1_bias: float32 [2, 768], P(None, ('head', 'blk'))
- grad_norm2_gain: float32 [2, 768], P(None, ('head', 'blk'))
- grad_norm2_bias: float32 [2, 768], P(None, ('head', 'blk'))
Inputs may be any that keep to these rules, and one draw needn't show every extreme that they name: lengths[i] is the number of valid leading positions of sequence i; in every draw one sequence has 1024 of them and one has 256. `slot_sequence`: a permutation of the sequences over the slots.
All inputs are finite; a program needn't handle non-finite values.
Results may differ from a plain program's by a relative error of at most 0.03.
Values may be sent and summed in bfloat16 or wider, within the bound.
A program may use at most 320 MiB of HBM per device.

v0:
```python
from functools import partial
import math

import jax
import jax.numpy as jnp
from jax import lax
from jax.sharding import PartitionSpec as P

H = 12
DH = 64
LAYERS = 2


EPS = 1e-05
NEG = -1e30


def dot_plain(former, latter):
    return jnp.dot(former, latter, preferred_element_type=jnp.float32)


def dot_right_t(former, latter):
    return lax.dot_general(
        former, latter, (((1,), (1,)), ((), ())), preferred_element_type=jnp.float32
    )


def dot_left_t(former, latter):
    return lax.dot_general(
        former, latter, (((0,), (0,)), ((), ())), preferred_element_type=jnp.float32
    )


def layer_norm(stream, factor, offset):
    centre = stream - jnp.mean(stream, axis=-1, keepdims=True)
    spread = lax.rsqrt(jnp.mean(centre * centre, axis=-1, keepdims=True) + EPS)
    normed = centre * spread
    return (normed * factor + offset, normed, spread)


def norm_back(upstream, normed, spread, factor):
    scaled = upstream * factor
    inner = (
        scaled
        - jnp.mean(scaled, axis=-1, keepdims=True)
        - normed * jnp.mean(scaled * normed, axis=-1, keepdims=True)
    )
    return (inner * spread, jnp.sum(upstream * normed, 0), jnp.sum(upstream, 0))


def pair_scores(queries, key_rows):
    return (
        jnp.einsum("sqhd,skhd->sqhk", queries, key_rows, preferred_element_type=jnp.float32) * 0.125
    )


def key_valid(start, count, slot_len):
    positions = start + lax.iota(jnp.int32, count)
    return (positions[None, :] < slot_len[:, None])[:, None, None, :]


def over_blocks(state, pieces, step_fn):
    width = pieces[0].shape[1]
    size = math.gcd(width, 512)

    def one_block(index, carry):
        offset = index * size
        parts = tuple((lax.dynamic_slice_in_dim(item, offset, size, 1) for item in pieces))
        return step_fn(carry, parts, offset)

    return lax.fori_loop(0, width // size, one_block, state)


def attention_forward(head_query, head_keys, head_values, slot_len):
    slots, rows, heads, _ = head_query.shape

    def max_step(carry, parts, start):
        peak, total = carry
        scores = jnp.where(
            key_valid(start, parts[0].shape[1], slot_len), pair_scores(head_query, parts[0]), NEG
        )
        top = jnp.maximum(peak, jnp.max(scores, -1))
        total = total * jnp.exp(peak - top) + jnp.sum(jnp.exp(scores - top[..., None]), -1)
        return (top, total)

    start_state = (
        jnp.full((slots, rows, heads), NEG, jnp.float32),
        jnp.zeros((slots, rows, heads), jnp.float32),
    )
    peak, total = over_blocks(
        start_state, (lax.all_gather(head_keys, "blk", axis=1, tiled=True),), max_step
    )
    log_norm = peak + jnp.log(total)

    def value_step(carry, parts, start):
        summed, fixed = carry
        key_part, value_part = parts
        scores = jnp.where(
            key_valid(start, key_part.shape[1], slot_len), pair_scores(head_query, key_part), NEG
        )
        probs = jnp.exp(scores - log_norm[..., None])
        rounded = probs.astype(jnp.bfloat16)
        remainder = (probs - rounded.astype(jnp.float32)).astype(jnp.bfloat16)
        summed = summed + jnp.einsum(
            "sqhk,skhd->sqhd", rounded, value_part, preferred_element_type=jnp.float32
        )
        fixed = fixed + jnp.einsum(
            "sqhk,skhd->sqhd", remainder, value_part, preferred_element_type=jnp.float32
        )
        return (summed, fixed)

    zeros = jnp.zeros(head_query.shape, jnp.float32)
    summed, fixed = over_blocks(
        (zeros, zeros),
        (
            lax.all_gather(head_keys, "blk", axis=1, tiled=True),
            lax.all_gather(head_values, "blk", axis=1, tiled=True),
        ),
        value_step,
    )
    return (log_norm, summed, summed + fixed)


def attention_backward(
    head_query, head_keys, head_values, back_heads, log_norm, delta, slot_len, own_valid
):

    def query_step(carry, parts, start):
        key_part, value_part = parts
        scores = jnp.where(
            key_valid(start, key_part.shape[1], slot_len), pair_scores(head_query, key_part), NEG
        )
        probs = jnp.exp(scores - log_norm[..., None])
        slope = jnp.einsum(
            "sqhd,skhd->sqhk", back_heads, value_part, preferred_element_type=jnp.float32
        )
        score_back = (probs * (slope - delta[..., None])).astype(jnp.bfloat16)
        return carry + jnp.einsum(
            "sqhk,skhd->sqhd", score_back, key_part, preferred_element_type=jnp.float32
        )

    zeros = jnp.zeros(head_query.shape, jnp.float32)
    query_sum = over_blocks(
        zeros,
        (
            lax.all_gather(head_keys, "blk", axis=1, tiled=True),
            lax.all_gather(head_values, "blk", axis=1, tiled=True),
        ),
        query_step,
    )
    all_log, all_delta = (
        lax.all_gather(log_norm, "blk", axis=1, tiled=True),
        lax.all_gather(delta, "blk", axis=1, tiled=True),
    )

    def key_step(carry, parts, start):
        key_sum, value_sum = carry
        query_part, back_part = parts
        count = query_part.shape[1]
        log_part = lax.dynamic_slice_in_dim(all_log, start, count, 1)
        delta_part = lax.dynamic_slice_in_dim(all_delta, start, count, 1)
        scores = jnp.where(own_valid, pair_scores(query_part, head_keys), NEG)
        probs = jnp.exp(scores - log_part[..., None])
        rounded = probs.astype(jnp.bfloat16)
        value_sum = value_sum + jnp.einsum(
            "sqhk,sqhd->skhd", rounded, back_part, preferred_element_type=jnp.float32
        )
        slope = jnp.einsum(
            "sqhd,skhd->sqhk", back_part, head_values, preferred_element_type=jnp.float32
        )
        score_back = (probs * (slope - delta_part[..., None])).astype(jnp.bfloat16)
        key_sum = key_sum + jnp.einsum(
            "sqhk,sqhd->skhd", score_back, query_part, preferred_element_type=jnp.float32
        )
        return (key_sum, value_sum)

    key_sum, value_sum = over_blocks(
        (zeros, zeros),
        (
            lax.all_gather(head_query, "blk", axis=1, tiled=True),
            lax.all_gather(back_heads, "blk", axis=1, tiled=True),
        ),
        key_step,
    )
    return (
        (query_sum * 0.125).astype(jnp.bfloat16),
        (key_sum * 0.125).astype(jnp.bfloat16),
        value_sum.astype(jnp.bfloat16),
    )


def fetch_forward(shards, layer_index):
    return (
        lax.all_gather(shards[0][layer_index], ("head", "blk"), axis=0, tiled=True),
        lax.all_gather(shards[1][layer_index], ("head", "blk"), axis=0, tiled=True),
        lax.all_gather(shards[2][layer_index], ("head", "blk"), axis=0, tiled=True),
        lax.all_gather(shards[3][layer_index], ("head", "blk"), axis=0, tiled=True),
        lax.all_gather(shards[4][layer_index], ("head", "blk"), axis=0, tiled=True),
        lax.all_gather(shards[5][layer_index], ("head", "blk"), axis=0, tiled=True),
        lax.all_gather(shards[6][layer_index], ("head", "blk"), axis=0, tiled=True),
        lax.all_gather(shards[7][layer_index], ("head", "blk"), axis=0, tiled=True),
        lax.all_gather(shards[8][layer_index], ("head", "blk"), axis=0, tiled=True),
        lax.all_gather(shards[9][layer_index], ("head", "blk"), axis=0, tiled=True),
        lax.all_gather(shards[10][layer_index], ("head", "blk"), axis=0, tiled=True),
        lax.all_gather(shards[11][layer_index], ("head", "blk"), axis=0, tiled=True),
        lax.all_gather(shards[12][layer_index], ("head", "blk"), axis=0, tiled=True),
        lax.all_gather(shards[13][layer_index], ("head", "blk"), axis=0, tiled=True),
        lax.all_gather(shards[14][layer_index], ("head", "blk"), axis=0, tiled=True),
    )


def fetch_backward(shards, layer_index):
    return (
        lax.all_gather(shards[0][layer_index], ("head", "blk"), axis=0, tiled=True),
        lax.all_gather(shards[1][layer_index], ("head", "blk"), axis=0, tiled=True),
        lax.all_gather(shards[2][layer_index], ("head", "blk"), axis=0, tiled=True),
        lax.all_gather(shards[3][layer_index], ("head", "blk"), axis=0, tiled=True),
        lax.all_gather(shards[4][layer_index], ("head", "blk"), axis=0, tiled=True),
        lax.all_gather(shards[5][layer_index], ("head", "blk"), axis=0, tiled=True),
        lax.all_gather(shards[6][layer_index], ("head", "blk"), axis=0, tiled=True),
        lax.all_gather(shards[7][layer_index], ("head", "blk"), axis=0, tiled=True),
        lax.all_gather(shards[8][layer_index], ("head", "blk"), axis=0, tiled=True),
        lax.all_gather(shards[9][layer_index], ("head", "blk"), axis=0, tiled=True),
        lax.all_gather(shards[10][layer_index], ("head", "blk"), axis=0, tiled=True),
        lax.all_gather(shards[11][layer_index], ("head", "blk"), axis=0, tiled=True),
        lax.all_gather(shards[12][layer_index], ("head", "blk"), axis=0, tiled=True),
        lax.all_gather(shards[13][layer_index], ("head", "blk"), axis=0, tiled=True),
        lax.all_gather(shards[14][layer_index], ("head", "blk"), axis=0, tiled=True),
    )


def pack_rows(terms, owners):
    rows = []
    shapes = []
    for term in terms:
        shapes.append((term.shape[0] // owners,) + term.shape[1:])
        flat = term.reshape(owners, -1)
        rows.append(flat)
    return (jnp.concatenate(rows, 1), shapes)


def unpack_row(summed, shapes):
    pieces = []
    offset = 0
    for shape in shapes:
        count = math.prod(shape)
        pieces.append(summed[0, offset : offset + count].reshape(shape))
        offset = offset + count
    return tuple(pieces)


def scatter_layer(terms, owners):
    packed, shapes = pack_rows(terms, owners)
    summed = lax.psum_scatter(packed, ("head", "blk"), scatter_dimension=0, tiled=True)
    return unpack_row(summed, shapes)


def per_device(
    tokens,
    lengths,
    slot_sequence,
    cotangent,
    w_query,
    w_key,
    w_value,
    w_out,
    w_in,
    w_down,
    b_query,
    b_value,
    b_out,
    b_in,
    b_down,
    norm1_gain,
    norm1_bias,
    norm2_gain,
    norm2_bias,
):
    slots_here, local, width = tokens.shape
    head_count = lax.axis_size("head")
    owners = head_count * lax.axis_size("blk")
    heads = H // head_count
    all_slots = lengths.shape[0]
    slot_ids = lax.iota(jnp.int32, all_slots)
    slot_len = jnp.sum(
        jnp.where(slot_sequence[:, None] == slot_ids[None, :], lengths[None, :], 0), axis=1
    )
    own_ids = lax.axis_index("head") * slots_here + lax.iota(jnp.int32, slots_here)
    own_len = jnp.sum(
        jnp.where(own_ids[:, None] == slot_ids[None, :], slot_len[None, :], 0), axis=1
    )
    token_pos = lax.axis_index("blk") * local + lax.iota(jnp.int32, local)
    row_valid = jnp.where(token_pos[None, :] < own_len[:, None], 1.0, 0.0).astype(jnp.float32)
    own_valid = key_valid(lax.axis_index("blk") * local, local, slot_len)
    shards = (
        w_query,
        w_key,
        w_value,
        w_out,
        w_in,
        w_down,
        b_query,
        b_value,
        b_out,
        b_in,
        b_down,
        norm1_gain,
        norm1_bias,
        norm2_gain,
        norm2_bias,
    )
    hidden = tokens.astype(jnp.float32)
    kept_list = []
    weight_list = []
    for layer_index in range(LAYERS):
        weights = fetch_forward(shards, layer_index)
        (
            forward_mat_query,
            forward_mat_key,
            forward_mat_value,
            forward_mat_out,
            forward_mat_in,
            forward_mat_down,
            forward_bias_query,
            forward_bias_value,
            forward_bias_out,
            forward_bias_in,
            forward_bias_down,
            forward_gain_one,
            forward_shift_one,
            forward_gain_two,
            forward_shift_two,
        ) = weights
        flat = hidden.reshape(slots_here * local, width)
        forward_inputs = flat.astype(jnp.bfloat16)
        queries = (dot_plain(forward_inputs, forward_mat_query) + forward_bias_query).astype(
            jnp.bfloat16
        )
        key_rows = dot_plain(forward_inputs, forward_mat_key).astype(jnp.bfloat16)
        value_rows = (dot_plain(forward_inputs, forward_mat_value) + forward_bias_value).astype(
            jnp.bfloat16
        )
        forward_stacked = jnp.stack([queries, key_rows, value_rows], 1).reshape(
            slots_here, local, 3, width
        )
        grouped = lax.all_to_all(forward_stacked, "head", split_axis=3, concat_axis=0, tiled=True)
        headed = grouped.reshape(all_slots, local, 3, heads, DH)
        forward_head_query = headed[:, :, 0]
        forward_head_keys = headed[:, :, 1]
        forward_head_values = headed[:, :, 2]
        forward_log_norm, summed, forward_exact = attention_forward(
            forward_head_query, forward_head_keys, forward_head_values, slot_len
        )
        context_head = summed.astype(jnp.bfloat16).reshape(all_slots, local, heads * DH)
        forward_context = lax.all_to_all(
            context_head, "head", split_axis=0, concat_axis=2, tiled=True
        ).reshape(slots_here * local, width)
        first = flat + dot_plain(forward_context, forward_mat_out) + forward_bias_out
        normed_one, forward_hat_one, forward_spread_one = layer_norm(
            first, forward_gain_one.astype(jnp.float32), forward_shift_one.astype(jnp.float32)
        )
        forward_ff_in = normed_one.astype(jnp.bfloat16)
        forward_pre_act = dot_plain(forward_ff_in, forward_mat_in) + forward_bias_in
        forward_activated = jax.nn.gelu(forward_pre_act, approximate=False).astype(jnp.bfloat16)
        second = normed_one + dot_plain(forward_activated, forward_mat_down) + forward_bias_down
        result, forward_hat_two, forward_spread_two = layer_norm(
            second, forward_gain_two.astype(jnp.float32), forward_shift_two.astype(jnp.float32)
        )
        forward_kept = (
            forward_inputs,
            forward_head_query,
            forward_head_keys,
            forward_head_values,
            forward_log_norm,
            forward_exact,
            forward_context,
            forward_hat_one,
            forward_spread_one,
            forward_ff_in,
            forward_pre_act,
            forward_activated,
            forward_hat_two,
            forward_spread_two,
        )
        hidden = result.reshape(slots_here, local, width)
        kept_list.append(forward_kept)
        weight_list.append(weights)
    back = (cotangent.astype(jnp.float32) * row_valid[:, :, None]).reshape(
        slots_here * local, width
    )
    grad_layers = [None] * LAYERS
    for layer_index in reversed(range(LAYERS)):
        weights = fetch_backward(shards, layer_index)
        (
            mat_query,
            mat_key,
            mat_value,
            mat_out,
            mat_in,
            mat_down,
            bias_query,
            bias_value,
            bias_out,
            bias_in,
            bias_down,
            gain_one,
            shift_one,
            gain_two,
            shift_two,
        ) = weights
        (
            inputs,
            head_query,
            head_keys,
            head_values,
            log_norm,
            exact,
            context,
            hat_one,
            spread_one,
            ff_in,
            pre_act,
            activated,
            hat_two,
            spread_two,
        ) = kept_list[layer_index]
        back_second, grad_gain_two, grad_shift_two = norm_back(
            back, hat_two, spread_two, gain_two.astype(jnp.float32)
        )
        back_down = back_second.astype(jnp.bfloat16)
        grad_mat_down = dot_left_t(activated, back_down)
        grad_bias_down = jnp.sum(back_down.astype(jnp.float32), 0)
        back_act = dot_right_t(back_down, mat_down)
        gelu_pull = jax.vjp(partial(jax.nn.gelu, approximate=False), pre_act)[1]
        back_pre = gelu_pull(back_act)[0].astype(jnp.bfloat16)
        grad_mat_in = dot_left_t(ff_in, back_pre)
        grad_bias_in = jnp.sum(back_pre.astype(jnp.float32), 0)
        back_normed = back_second + dot_right_t(back_pre, mat_in)
        back_first, grad_gain_one, grad_shift_one = norm_back(
            back_normed, hat_one, spread_one, gain_one.astype(jnp.float32)
        )
        back_branch = back_first.astype(jnp.bfloat16)
        grad_mat_out = dot_left_t(context, back_branch)
        grad_bias_out = jnp.sum(back_branch.astype(jnp.float32), 0)
        back_context = (
            dot_right_t(back_branch, mat_out).astype(jnp.bfloat16).reshape(slots_here, local, width)
        )
        back_heads = lax.all_to_all(
            back_context, "head", split_axis=2, concat_axis=0, tiled=True
        ).reshape(all_slots, local, heads, DH)
        delta = jnp.sum(back_heads.astype(jnp.float32) * exact, -1)
        query_back, key_back, value_back = attention_backward(
            head_query, head_keys, head_values, back_heads, log_norm, delta, slot_len, own_valid
        )
        stacked = jnp.stack([query_back, key_back, value_back], 2).reshape(
            all_slots, local, 3, heads * DH
        )
        joined = lax.all_to_all(stacked, "head", split_axis=0, concat_axis=3, tiled=True).reshape(
            slots_here * local, 3, width
        )
        back_query = joined[:, 0]
        back_key = joined[:, 1]
        back_value = joined[:, 2]
        grad_mat_query = dot_left_t(inputs, back_query)
        grad_mat_key = dot_left_t(inputs, back_key)
        grad_mat_value = dot_left_t(inputs, back_value)
        grad_bias_query = jnp.sum(back_query.astype(jnp.float32), 0)
        grad_bias_value = jnp.sum(back_value.astype(jnp.float32), 0)
        back_hidden = (
            back_first
            + dot_right_t(back_query, mat_query)
            + dot_right_t(back_key, mat_key)
            + dot_right_t(back_value, mat_value)
        )
        terms = (
            grad_mat_query,
            grad_mat_key,
            grad_mat_value,
            grad_mat_out,
            grad_mat_in,
            grad_mat_down,
            grad_bias_query,
            grad_bias_value,
            grad_bias_out,
            grad_bias_in,
            grad_bias_down,
            grad_gain_one,
            grad_shift_one,
            grad_gain_two,
            grad_shift_two,
        )
        back, terms = (back_hidden, terms)
        grad_layers[layer_index] = scatter_layer(terms, owners)
    grads = tuple(
        (jnp.stack([grad_layers[index][member] for index in range(LAYERS)]) for member in range(15))
    )
    return (hidden, back.reshape(slots_here, local, width)) + tuple(grads)


def solution(mesh):
    placed = (
        P("head", "blk", None),
        P(),
        P(),
        P("head", "blk", None),
        P(None, ("head", "blk"), None),
        P(None, ("head", "blk"), None),
        P(None, ("head", "blk"), None),
        P(None, ("head", "blk"), None),
        P(None, ("head", "blk"), None),
        P(None, ("head", "blk"), None),
        P(None, ("head", "blk")),
        P(None, ("head", "blk")),
        P(None, ("head", "blk")),
        P(None, ("head", "blk")),
        P(None, ("head", "blk")),
        P(None, ("head", "blk")),
        P(None, ("head", "blk")),
        P(None, ("head", "blk")),
        P(None, ("head", "blk")),
    )
    return jax.shard_map(
        per_device,
        mesh=mesh,
        in_specs=placed,
        out_specs=(
            P("head", "blk", None),
            P("head", "blk", None),
            P(None, ("head", "blk"), None),
            P(None, ("head", "blk"), None),
            P(None, ("head", "blk"), None),
            P(None, ("head", "blk"), None),
            P(None, ("head", "blk"), None),
            P(None, ("head", "blk"), None),
            P(None, ("head", "blk")),
            P(None, ("head", "blk")),
            P(None, ("head", "blk")),
            P(None, ("head", "blk")),
            P(None, ("head", "blk")),
            P(None, ("head", "blk")),
            P(None, ("head", "blk")),
            P(None, ("head", "blk")),
            P(None, ("head", "blk")),
        ),
        check_vma=False,
    )
```

profile of v0, /device:TPU:0, one launch (start us, length us, event | category | flops | bytes accessed | tf_op | source)
XLA Modules:
  0.0 2391.1 jit_solution(10942623257777453733)
XLA Ops:
  32.3 43.8 %all-reduce.21 = (bf16[3072]{0:T(1024)(128)(2,1)}, bf16[3072]{0:T(1024)(128)(2,1)S(1)}, bf16[768]{0:T(1024)(128)(2,1)}, bf16[768]{0:T(1024)(128)(2,1)S(1)}, bf16...) all-reduce(bf16[3072]{0:T(1024)(128)(2,1)S(1)} %dynamic-update-slic, ...), channel_id=31, replica_groups=mesh['head'=4,'blk'=8] {'head','blk'}, use_global_device_ids=true, to_apply=%add.14 | all-reduce | flops 18432 | bytes 73728
  78.4 46.7 %all-gather.63.cloned.1.call-done = bf16[1,768,768]{2,1,0:T(8,128)(2,1)} async-done(((bf16[1,24,768]{2,1,0:T(8,128)(2,1)}), bf16[1,768,768]{2,1,0:T(8,128)(2,1)}) %all-gather.63.cloned.1.call-update) | async-done | bytes 1179664 | tf_op jit(solution)/shard_map/all_gather | solution.py:195
  127.4 54.4 %all-gather.61.cloned.1.call-done = bf16[1,768,768]{2,1,0:T(8,128)(2,1)} async-done(((bf16[1,24,768]{2,1,0:T(8,128)(2,1)}), bf16[1,768,768]{2,1,0:T(8,128)(2,1)}) %all-gather.61.cloned.1.call-update) | async-done | bytes 1179664 | tf_op jit(solution)/shard_map/all_gather | solution.py:194
  185.8 18.3 all_to_all.120
  210.6 57.5 %all-gather.69.cloned.1.call-done = bf16[8,1024,1,3,64]{1,4,3,2,0:T(8,128)(2,1)} async-done(((bf16[8,128,1,3,64]{1,4,3,2,0:T(8,128)(2,1)}), bf16[8,1024,1,3,64]{1,4,3,2,0:T(8,128)(2,1)}) %all-gather.69.cloned.1.call-update) | async-done | bytes 3145744 | tf_op jit(solution)/shard_map/all_gather | solution.py:116
  268.2 17.0 while.124
  285.8 45.5 %all-gather.67.cloned.1.call-done = bf16[8,1024,1,3,64]{1,4,3,2,0:T(8,128)(2,1)} async-done(((bf16[8,128,1,3,64]{1,4,3,2,0:T(8,128)(2,1)}), bf16[8,1024,1,3,64]{1,4,3,2,0:T(8,128)(2,1)}) %all-gather.67.cloned.1.call-update) | async-done | bytes 3145744 | tf_op jit(solution)/shard_map/all_gather | solution.py:117
  331.3 29.5 %while.125 = (s32[]{:T(128)}, f32[8,128,3,64]{1,3,2,0:T(8,128)}, f32[8,128,3,64]{1,3,2,0:T(8,128)}, bf16[8,1024,3,64]{1,3,2,0:T(8,128)(2,1)}, s32[8]{0:T(128)S(1...) while((s32[]{:T(128)}, f32[8,128,3,64]{1,3,2,0:T(8,128)}, ...), condition=%wide.region_6.7_spmd.clone, body=%wide.region_5.6_spmd.clone.sunk | while | flops 622072320 | bytes 71266672 | solution.py:71
  374.2 12.4 all-gather.71.cloned.1.call-done
  388.9 63.8 %all-gather.73.cloned.1.call-done = bf16[1,768,3072]{2,1,0:T(8,128)(2,1)} async-done(((bf16[1,24,3072]{2,1,0:T(8,128)(2,1)}), bf16[1,768,3072]{2,1,0:T(8,128)(2,1)}) %all-gather.73.cloned.1.call-update) | async-done | bytes 4718608 | tf_op jit(solution)/shard_map/all_gather | solution.py:198
  452.7 11.3 multiply_convert_fusion.1
  464.0 54.7 %all-gather.75.cloned.1.call-done = bf16[1,3072,768]{2,1,0:T(8,128)(2,1)} async-done(((bf16[1,96,768]{2,1,0:T(8,128)(2,1)}), bf16[1,3072,768]{2,1,0:T(8,128)(2,1)}) %all-gather.75.cloned.1.call-update) | async-done | bytes 4718608 | tf_op jit(solution)/shard_map/all_gather | solution.py:199
  523.7 51.0 %all-gather.81.cloned.1.call-done = bf16[1,768,768]{2,1,0:T(8,128)(2,1)} async-done(((bf16[1,24,768]{2,1,0:T(8,128)(2,1)}), bf16[1,768,768]{2,1,0:T(8,128)(2,1)}) %all-gather.81.cloned.1.call-update) | async-done | bytes 1179664 | tf_op jit(solution)/shard_map/all_gather | solution.py:196
  576.9 53.7 %all-gather.79.cloned.1.call-done = bf16[1,768,768]{2,1,0:T(8,128)(2,1)} async-done(((bf16[1,24,768]{2,1,0:T(8,128)(2,1)}), bf16[1,768,768]{2,1,0:T(8,128)(2,1)}) %all-gather.79.cloned.1.call-update) | async-done | bytes 1179664 | tf_op jit(solution)/shard_map/all_gather | solution.py:195
  632.7 53.8 %all-gather.77.cloned.1.call-done = bf16[1,768,768]{2,1,0:T(8,128)(2,1)} async-done(((bf16[1,24,768]{2,1,0:T(8,128)(2,1)}), bf16[1,768,768]{2,1,0:T(8,128)(2,1)}) %all-gather.77.cloned.1.call-update) | async-done | bytes 1179664 | tf_op jit(solution)/shard_map/all_gather | solution.py:194
  690.6 18.3 all_to_all.121
  712.7 11.9 all-gather.91.cloned.1.call-start
  725.6 47.2 %all-gather.85.cloned.1.call-done = bf16[8,1024,1,3,64]{1,4,3,2,0:T(8,128)(2,1)} async-done(((bf16[8,128,1,3,64]{1,4,3,2,0:T(8,128)(2,1)}), bf16[8,1024,1,3,64]{1,4,3,2,0:T(8,128)(2,1)}) %all-gather.85.cloned.1.call-update) | async-done | bytes 3145744 | tf_op jit(solution)/shard_map/all_gather | solution.py:116
  772.9 17.0 while.126
  790.5 45.7 %all-gather.83.cloned.1.call-done = bf16[8,1024,1,3,64]{1,4,3,2,0:T(8,128)(2,1)} async-done(((bf16[8,128,1,3,64]{1,4,3,2,0:T(8,128)(2,1)}), bf16[8,1024,1,3,64]{1,4,3,2,0:T(8,128)(2,1)}) %all-gather.83.cloned.1.call-update) | async-done | bytes 3145744 | tf_op jit(solution)/shard_map/all_gather | solution.py:117
  836.2 29.5 %while.127 = (s32[]{:T(128)}, f32[8,128,3,64]{1,3,2,0:T(8,128)}, f32[8,128,3,64]{1,3,2,0:T(8,128)}, bf16[8,1024,3,64]{1,3,2,0:T(8,128)(2,1)}, s32[8]{0:T(128)S(1...) while((s32[]{:T(128)}, f32[8,128,3,64]{1,3,2,0:T(8,128)}, ...), condition=%wide.region_16.17_spmd.clone, body=%wide.region_15.16_spmd.clone.sunk | while | flops 622072320 | bytes 71266672 | solution.py:71
  879.0 12.5 all-gather.87.cloned.1.call-done
  893.7 63.7 %all-gather.89.cloned.1.call-done = bf16[1,768,3072]{2,1,0:T(8,128)(2,1)} async-done(((bf16[1,24,3072]{2,1,0:T(8,128)(2,1)}), bf16[1,768,3072]{2,1,0:T(8,128)(2,1)}) %all-gather.89.cloned.1.call-update) | async-done | bytes 4718608 | tf_op jit(solution)/shard_map/all_gather | solution.py:198
  957.4 11.6 multiply_convert_fusion
  969.0 54.2 %all-gather.91.cloned.1.call-done = bf16[1,3072,768]{2,1,0:T(8,128)(2,1)} async-done(((bf16[1,96,768]{2,1,0:T(8,128)(2,1)}), bf16[1,3072,768]{2,1,0:T(8,128)(2,1)}) %all-gather.91.cloned.1.call-update) | async-done | bytes 4718608 | tf_op jit(solution)/shard_map/all_gather | solution.py:199
  1038.3 9.9 all_to_all.122
  1050.4 28.7 %all_gather.187 = f32[8,1024,3]{1,2,0:T(4,128)} all-gather(f32[8,128,3]{1,2,0:T(4,128)S(1)} %copy-done.67), channel_id=1, replica_groups=mesh['head'=4,'blk'=8] {'blk'}, dimensions={1}, use_global_device_ids=true | all-gather | bytes 110592 | tf_op jit(solution)/shard_map/all_gather | solution.py:152
  1079.0 30.4 %all_gather.183 = f32[8,1024,3]{1,2,0:T(4,128)} all-gather(f32[8,128,3]{1,2,0:T(4,128)S(1)} %copy-done.69), channel_id=1, replica_groups=mesh['head'=4,'blk'=8] {'blk'}, dimensions={1}, use_global_device_ids=true | all-gather | bytes 110592 | tf_op jit(solution)/shard_map/all_gather | solution.py:152
  1116.1 27.9 %all_gather.185 = f32[8,1024,3]{1,2,0:T(4,128)} all-gather(f32[8,128,3]{1,2,0:T(4,128)S(1)} %multiply_reduce_fusion.6), channel_id=1, replica_groups=mesh['head'=4,'blk'=8] {'blk'}, dimensions={1}, use_global_device_ids=true | all-gather | bytes 110592 | tf_op jit(solution)/shard_map/all_gather | solution.py:153
  1144.0 24.3 %while.128 = (s32[]{:T(128)}, f32[8,128,3,64]{1,3,2,0:T(8,128)}, bf16[8,1024,3,64]{1,3,2,0:T(8,128)(2,1)S(1)}, s32[8]{0:T(128)S(1)}, bf16[8,128,3,64]{1,3,2,0:T(...) while((s32[]{:T(128)}, f32[8,128,3,64]{1,3,2,0:T(8,128)}, ...), condition=%wide.region_28.29_spmd.clone, body=%wide.region_27.28_spmd.clone.sunk | while | flops 613814784 | bytes 19699428 | solution.py:71
  1161.0 7.2 fusion.524
  1170.3 39.7 %while.129 = (s32[]{:T(128)}, f32[8,128,3,64]{1,3,2,0:T(8,128)}, f32[8,128,3,64]{1,3,2,0:T(8,128)}, bf16[8,1024,3,64]{1,3,2,0:T(8,128)(2,1)}, bf16[8,128,3,64]{1...) while((s32[]{:T(128)}, f32[8,128,3,64]{1,3,2,0:T(8,128)}, ...), condition=%wide.region_30.31_spmd.clone, body=%wide.region_29.30_spmd.clone.sunk | while | flops 821822464 | bytes 42851688 | solution.py:71
  1175.7 8.8 fusion.534
  1195.4 8.9 fusion.534
  1224.9 8.1 reshape.623
  1239.6 8.2 reshape.624
  1300.2 7.8 constant_dynamic-update-slice_fusion.7
  1308.8 7.9 constant_dynamic-update-slice_fusion.6
  1325.3 28.0 %all_gather.189 = f32[8,1024,3]{1,2,0:T(4,128)} all-gather(f32[8,128,3]{1,2,0:T(4,128)S(1)} %multiply_reduce_fusion.3), channel_id=1, replica_groups=mesh['head'=4,'blk'=8] {'blk'}, dimensions={1}, use_global_device_ids=true | all-gather | bytes 110592 | tf_op jit(solution)/shard_map/all_gather | solution.py:153
  1353.3 24.3 %while.130 = (s32[]{:T(128)}, f32[8,128,3,64]{1,3,2,0:T(8,128)}, bf16[8,1024,3,64]{1,3,2,0:T(8,128)(2,1)S(1)}, s32[8]{0:T(128)S(1)}, bf16[8,128,3,64]{1,3,2,0:T(...) while((s32[]{:T(128)}, f32[8,128,3,64]{1,3,2,0:T(8,128)}, ...), condition=%wide.region_37.38_spmd.clone, body=%wide.region_36.37_spmd.clone.sunk | while | flops 613814784 | bytes 19699428 | solution.py:71
  1370.7 6.9 fusion.543
  1379.6 39.5 %while.131 = (s32[]{:T(128)}, f32[8,128,3,64]{1,3,2,0:T(8,128)}, f32[8,128,3,64]{1,3,2,0:T(8,128)}, bf16[8,1024,3,64]{1,3,2,0:T(8,128)(2,1)}, bf16[8,128,3,64]{1...) while((s32[]{:T(128)}, f32[8,128,3,64]{1,3,2,0:T(8,128)}, ...), condition=%wide.region_39.40_spmd.clone, body=%wide.region_38.39_spmd.clone.sunk | while | flops 821822464 | bytes 42849612 | solution.py:71
  1385.0 8.7 fusion.553
  1404.5 8.9 fusion.553
  1434.1 8.3 reshape.608
  1449.1 8.2 reshape.609
  1520.8 8.5 constant_dynamic-update-slice_fusion.1
  1552.1 805.1 %all-reduce.24.cloned.1.call-done = (f32[32,221472]{1,0:T(8,128)}, f32[32,221472]{1,0:T(8,128)}) async-done(((f32[32,221472]{1,0:T(8,128)}, f32[32,221472]{1,0:T(8,128)}), (f32[32,221472]{1,0:T(8,128)}, f32[32,221472]{1,0:T(8,128)})) %all-reduce.24.cloned.1.call-update) | async-done | bytes 56696848
  (755 shorter events, 505.0 us)
Async XLA Ops:
  7.2 118.0 %copy-start.28 = (bf16[2,128,768]{2,1,0:T(8,128)(2,1)S(1)}, bf16[2,128,768]{2,1,0:T(8,128)(2,1)}, u32[]{:S(2)}) copy-start(bf16[2,128,768]{2,1,0:T(8,128)(2,1)} %param.35) | copy-start | bytes 1179652
  7.2 68.9 %all-gather.65.cloned.1.call-start = ((), (), s32[]{:S(2)}) async-start(), calls=%async_computation.12 | async-start | bytes 1216512 | tf_op jit(solution)/shard_map/all_gather | solution.py:196
  8.7 116.5 %all-gather.63.cloned.1.call-start = ((), (), s32[]{:S(2)}) async-start(), calls=%async_computation.11 | async-start | bytes 1216512 | tf_op jit(solution)/shard_map/all_gather | solution.py:195
  10.2 171.5 %all-gather.61.cloned.1.call-start = ((), (), s32[]{:S(2)}) async-start(), calls=%async_computation.10 | async-start | bytes 1216512 | tf_op jit(solution)/shard_map/all_gather | solution.py:194
  11.7 256.4 %all-gather.69.cloned.1.call-start = ((), (), s32[]{:S(2)}) async-start(), calls=%async_computation.14 | async-start | bytes 3538944 | tf_op jit(solution)/shard_map/all_gather | solution.py:116
  206.1 125.2 %all-gather.67.cloned.1.call-start = ((), (), s32[]{:S(2)}) async-start(), calls=%async_computation.13 | async-start | bytes 3538944 | tf_op jit(solution)/shard_map/all_gather | solution.py:117
  206.7 180.0 %all-gather.71.cloned.1.call-start = ((), (), s32[]{:S(2)}) async-start(), calls=%async_computation.15 | async-start | bytes 1216512 | tf_op jit(solution)/shard_map/all_gather | solution.py:197
  207.4 245.3 %all-gather.73.cloned.1.call-start = ((), (), s32[]{:S(2)}) async-start(), calls=%async_computation.16 | async-start | bytes 4866048 | tf_op jit(solution)/shard_map/all_gather | solution.py:198
  208.2 310.5 %all-gather.75.cloned.1.call-start = ((), (), s32[]{:S(2)}) async-start(), calls=%async_computation.17 | async-start | bytes 4866048 | tf_op jit(solution)/shard_map/all_gather | solution.py:199
  209.0 365.6 %all-gather.81.cloned.1.call-start = ((), (), s32[]{:S(2)}) async-start(), calls=%async_computation.20 | async-start | bytes 1216512 | tf_op jit(solution)/shard_map/all_gather | solution.py:196
  209.8 420.7 %all-gather.79.cloned.1.call-start = ((), (), s32[]{:S(2)}) async-start(), calls=%async_computation.19 | async-start | bytes 1216512 | tf_op jit(solution)/shard_map/all_gather | solution.py:195
  362.9 10.9 all-to-all-start.1
  366.4 320.1 %all-gather.77.cloned.1.call-start = ((), (), s32[]{:S(2)}) async-start(), calls=%async_computation.18 | async-start | bytes 1216512 | tf_op jit(solution)/shard_map/all_gather | solution.py:194
  367.1 405.7 %all-gather.85.cloned.1.call-start = ((), (), s32[]{:S(2)}) async-start(), calls=%async_computation.22 | async-start | bytes 3538944 | tf_op jit(solution)/shard_map/all_gather | solution.py:116
  369.2 149.5 %copy-start.61 = (f32[768]{0:T(1024)}, f32[768]{0:T(1024)S(1)}, u32[]{:S(2)}) copy-start(f32[768]{0:T(1024)S(1)} %convert_element_type.347) | copy-start | bytes 9220
  369.9 148.8 %copy-start.59 = (f32[768]{0:T(1024)}, f32[768]{0:T(1024)S(1)}, u32[]{:S(2)}) copy-start(f32[768]{0:T(1024)S(1)} %convert_element_type.346) | copy-start | bytes 9220
  370.6 152.3 %copy-start.105 = (f32[768]{0:T(1024)}, f32[768]{0:T(1024)S(1)}, u32[]{:S(2)}) copy-start(f32[768]{0:T(1024)S(1)} %convert_element_type.351) | copy-start | bytes 9220
  371.3 151.6 %copy-start.87 = (f32[768]{0:T(1024)}, f32[768]{0:T(1024)S(1)}, u32[]{:S(2)}) copy-start(f32[768]{0:T(1024)S(1)} %convert_element_type.350) | copy-start | bytes 9220
  388.6 130.1 %copy-start.23 = (f32[256,768]{1,0:T(8,128)}, f32[256,768]{1,0:T(8,128)S(1)}, u32[]{:S(2)}) copy-start(f32[256,768]{1,0:T(8,128)S(1)} %get-tuple-element.1770) | copy-start | bytes 2359300
  388.6 130.1 %copy-start.94 = (f32[256]{0:T(256)}, f32[256]{0:T(256)S(1)}, u32[]{:S(2)}) copy-start(f32[256]{0:T(256)S(1)} %broadcast_multiply_fusion.10) | copy-start | bytes 3076
  388.9 129.9 %copy-start.111 = (f32[256]{0:T(256)}, f32[256]{0:T(256)S(1)}, u32[]{:S(2)}) copy-start(f32[256]{0:T(256)S(1)} %add_rsqrt_fusion.3) | copy-start | bytes 3076
  464.0 58.5 %copy-start.37 = (bf16[256,3072]{1,0:T(8,128)(2,1)}, bf16[256,3072]{1,0:T(8,128)(2,1)S(1)}, u32[]{:S(2)}) copy-start(bf16[256,3072]{1,0:T(8,128)(2,1)S(1)} %get-tuple-element.1695) | copy-start | bytes 4718596
  522.6 109.7 %copy-start.92 = (f32[256]{0:T(256)}, f32[256]{0:T(256)S(1)}, u32[]{:S(2)}) copy-start(f32[256]{0:T(256)S(1)} %broadcast_multiply_fusion.9) | copy-start | bytes 3076
  523.5 109.3 %copy-start.109 = (f32[256]{0:T(256)}, f32[256]{0:T(256)S(1)}, u32[]{:S(2)}) copy-start(f32[256]{0:T(256)S(1)} %add_rsqrt_fusion.2) | copy-start | bytes 3076
  523.7 164.6 %copy-start.17 = (bf16[256,768]{1,0:T(8,128)(2,1)}, bf16[256,768]{1,0:T(8,128)(2,1)S(1)}, u32[]{:S(2)}) copy-start(bf16[256,768]{1,0:T(8,128)(2,1)S(1)} %fusion.338) | copy-start | bytes 1179652
  710.8 125.4 %all-gather.83.cloned.1.call-start = ((), (), s32[]{:S(2)}) async-start(), calls=%async_computation.21 | async-start | bytes 3538944 | tf_op jit(solution)/shard_map/all_gather | solution.py:117
  711.6 180.0 %all-gather.87.cloned.1.call-start = ((), (), s32[]{:S(2)}) async-start(), calls=%async_computation.23 | async-start | bytes 1216512 | tf_op jit(solution)/shard_map/all_gather | solution.py:197
  712.1 245.3 %all-gather.89.cloned.1.call-start = ((), (), s32[]{:S(2)}) async-start(), calls=%async_computation.24 | async-start | bytes 4866048 | tf_op jit(solution)/shard_map/all_gather | solution.py:198
  712.7 310.5 %all-gather.91.cloned.1.call-start = ((), (), s32[]{:S(2)}) async-start(), calls=%async_computation.25 | async-start | bytes 4866048 | tf_op jit(solution)/shard_map/all_gather | solution.py:199
  724.8 48.1 %copy-start.89 = (s32[128]{0:T(128)}, s32[128]{0:T(128)S(1)}, u32[]{:S(2)}) copy-start(s32[128]{0:T(128)S(1)} %iota_add_fusion.7) | copy-start | bytes 1540
  867.7 10.9 all-to-all-start.3
  871.2 299.1 %all-gather.93.cloned.1.call-start = ((), (), s32[]{:S(2)}) async-start(), calls=%async_computation.26 | async-start | bytes 3538944 | tf_op jit(solution)/shard_map/all_gather | solution.py:180
  876.1 294.1 %all-gather.57.cloned.1.call-start = ((), (), s32[]{:S(2)}) async-start(), calls=%async_computation.8 | async-start | bytes 3538944 | tf_op jit(solution)/shard_map/all_gather | solution.py:181
  879.0 90.0 %copy-start.44 = (bf16[2,128,4,192]{1,0,3,2:T(2,128)(2,1)}, bf16[2,128,4,192]{1,0,3,2:T(2,128)(2,1)S(1)}, u32[]{:S(2)}) copy-start(bf16[2,128,4,192]{1,0,3,2:T(2,128)(2,1)S(1)} %copy.207) | copy-start | bytes 1179652
  879.0 78.4 %copy-start.118 = (f32[3072]{0:T(1024)S(1)}, f32[3072]{0:T(1024)}, u32[]{:S(2)}) copy-start(f32[3072]{0:T(1024)} %convert_element_type.357) | copy-start | bytes 36868
  893.4 142.3 %copy-start.26 = (f32[256,768]{1,0:T(8,128)}, f32[256,768]{1,0:T(8,128)S(1)}, u32[]{:S(2)}) copy-start(f32[256,768]{1,0:T(8,128)S(1)} %get-tuple-element.1775) | copy-start | bytes 2359300
  893.4 140.1 %copy-start.97 = (f32[256]{0:T(256)}, f32[256]{0:T(256)S(1)}, u32[]{:S(2)}) copy-start(f32[256]{0:T(256)S(1)} %broadcast_multiply_fusion.8) | copy-start | bytes 3076
  893.7 139.8 %copy-start.114 = (f32[256]{0:T(256)}, f32[256]{0:T(256)S(1)}, u32[]{:S(2)}) copy-start(f32[256]{0:T(256)S(1)} %add_rsqrt_fusion.1) | copy-start | bytes 3076
  893.7 129.6 %copy-start.125 = (f32[768]{0:T(1024)S(1)}, f32[768]{0:T(1024)}, u32[]{:S(2)}) copy-start(f32[768]{0:T(1024)} %convert_element_type.358) | copy-start | bytes 9220
  1037.3 72.1 %copy-start.12 = (f32[256,768]{1,0:T(8,128)}, f32[256,768]{1,0:T(8,128)S(1)}, u32[]{:S(2)}) copy-start(f32[256,768]{1,0:T(8,128)S(1)} %get-tuple-element.1692) | copy-start | bytes 2359300
  1037.3 72.1 %copy-start.45 = (bf16[2,128,4,192]{1,0,3,2:T(2,128)(2,1)S(1)}, bf16[2,128,4,192]{1,0,3,2:T(2,128)(2,1)}, u32[]{:S(2)}) copy-start(bf16[2,128,4,192]{1,0,3,2:T(2,128)(2,1)} %copy-done.44) | copy-start | bytes 1179652
  1049.1 330.4 %all-gather.95.cloned.1.call-start = ((), (), s32[]{:S(2)}) async-start(), calls=%async_computation.27 | async-start | bytes 3538944 | tf_op jit(solution)/shard_map/all_gather | solution.py:180
  1214.7 37.2 %all-to-all-start.5 = ((bf16[8,128,3,192]{1,3,2,0:T(8,128)(2,1)}), bf16[8,128,3,192]{1,3,2,0:T(8,128)(2,1)S(1)}, u32[]{:S(2)}, u32[]{:S(2)}) async-start(bf16[8,128,3,192]{1,3,2,0:T(8,128)(2,1)} %pad_maximum_fusion.2), calls=%async_computation.5 | async-start | bytes 2359296 | tf_op jit(solution)/shard_map/all_to_all | solution.py:458
  1275.8 42.9 %copy-start.10 = (f32[256,768]{1,0:T(8,128)}, f32[256,768]{1,0:T(8,128)S(1)}, u32[]{:S(2)}) copy-start(f32[256,768]{1,0:T(8,128)S(1)} %get-tuple-element.1688) | copy-start | bytes 2359300
  1277.4 30.5 %all-to-all-start.6 = ((bf16[2,128,768]{1,0,2:T(2,128)(2,1)}), bf16[2,128,768]{1,0,2:T(2,128)(2,1)S(1)}, u32[]{:S(2)}, u32[]{:S(2)}) async-start(bf16[2,128,768]{1,0,2:T(2,128)(2,1)} %copy.215), calls=%async_computation.6 | async-start | bytes 786432 | tf_op jit(solution)/shard_map/all_to_all | solution.py:448
  1280.9 98.7 %all-gather.59.cloned.1.call-start = ((), (), s32[]{:S(2)}) async-start(), calls=%async_computation.9 | async-start | bytes 3538944 | tf_op jit(solution)/shard_map/all_gather | solution.py:181
  1423.8 51.1 %all-to-all-start.7 = ((bf16[8,128,3,192]{1,3,2,0:T(8,128)(2,1)}), bf16[8,128,3,192]{1,3,2,0:T(8,128)(2,1)S(1)}, u32[]{:S(2)}, u32[]{:S(2)}) async-start(bf16[8,128,3,192]{1,3,2,0:T(8,128)(2,1)} %pad_maximum_fusion.3), calls=%async_computation.7 | async-start | bytes 2359296 | tf_op jit(solution)/shard_map/all_to_all | solution.py:458
  1427.3 929.8 %all-reduce.24.cloned.1.call-start = ((), (), s32[]{:S(2)}) async-start(), calls=%async_computation.28 | async-start | bytes 113442816
  (142 other events, 1210.7 us)
Sparse Core Ops, SparseCore 0:
  11.5 57.0 all-gather.64
  72.1 53.0 all-gather.62
  128.7 53.0 all-gather.60
  206.2 61.8 all-gather.68
  270.0 61.2 all-gather.66
  334.1 52.5 all-gather.70
  390.1 62.5 all-gather.72
  456.2 62.4 all-gather.74
  521.6 52.9 all-gather.80
  577.4 53.0 all-gather.78
  633.4 53.0 all-gather.76
  710.9 61.8 all-gather.84
  774.9 61.2 all-gather.82
  838.9 52.5 all-gather.86
  894.8 62.5 all-gather.88
  960.8 62.4 all-gather.90
  1025.2 63.6 all-gather.92
  1090.8 63.6 all-gather.56
  1156.5 61.3 all-gather.94
  1309.0 64.9 all-gather.58
  1547.3 809.8 all-reduce.23
where the time goes:
time: 2400 us; the launch traced here: 2390 us
  waiting for transfers between devices  1530 us (64%)
  matrix products  306 us (13%)
  local copies, waits for them, and re-layouts  229 us (10%)
  blocking collectives  205 us (9%)
  other arithmetic  73.1 us (3%)
  starting transfers between devices  30.8 us (1%)
    unnamed x22, waiting for transfers between devices  809 us
    all_gather x2, waiting for transfers between devices, fetch_forward(): lax.all_gather(shards[4][layer_index], ('head', 'blk'), axis=0, tiled=True)  128 us
    all_gather x2, waiting for transfers between devices, fetch_forward(): lax.all_gather(shards[5][layer_index], ('head', 'blk'), axis=0, tiled=True)  109 us
    all_gather x2, waiting for transfers between devices, fetch_forward(): lax.all_gather(shards[0][layer_index], ('head', 'blk'), axis=0, tiled=True)  108 us
    all_gather x2, waiting for transfers between devices, attention_forward(): lax.all_gather(head_keys, 'blk', axis=1, tiled=True)  105 us
    all_gather x2, waiting for transfers between devices, fetch_forward(): lax.all_gather(shards[1][layer_index], ('head', 'blk'), axis=0, tiled=True)  100 us
    unnamed x333, local copies, waits for them, and re-layouts  96.2 us
    all_gather x2, waiting for transfers between devices, attention_forward(): lax.all_gather(head_values, 'blk', axis=1, tiled=True)  91.2 us
  transfers between devices with their start and end apart: 26, of which 18 were waited for; matrix products, arithmetic and copies ran while one was open for 19% of the time, Pallas kernels for 0%

commit v1 on v0

--- a/solution.py
+++ b/solution.py
@@ -4,7 +4,9 @@
 import jax
 import jax.numpy as jnp
 from jax import lax
-from jax.sharding import PartitionSpec as P
+from jax.experimental import pallas as pl
+from jax.experimental.pallas import tpu as pltpu
+from jax.sharding import Mesh, PartitionSpec as P
 
 H = 12
 DH = 64
@@ -497,7 +499,7 @@
     return (hidden, back.reshape(slots_here, local, width)) + tuple(grads)
 
 
-def solution(mesh):
+def plain_solution(mesh):
     placed = (
         P("head", "blk", None),
         P(),
@@ -544,3 +546,659 @@
         ),
         check_vma=False,
     )
+
+
+MESH_ID = pl.DeviceIdType.MESH
+AXES = ("x", "c", "z", "y")
+NX, NC, NZ, NY = 2, 2, 4, 2
+F32 = jnp.float32
+BF16 = jnp.bfloat16
+
+
+def place():
+    return tuple(lax.axis_index(name) for name in AXES)
+
+
+class Sems:
+    def __init__(self, ref):
+        self.ref = ref
+        self.used = 0
+
+    def take(self):
+        self.used += 1
+        return self.ref.at[self.used - 1]
+
+
+def enter_barrier():
+    x, c, z, y = place()
+    barrier = pltpu.get_barrier_semaphore()
+    peers = [(1 - x, c, z, y), (x, c, z, 1 - y)]
+    for dz in range(NZ):
+        for dc in range(NC):
+            if dz or dc:
+                peers.append((x, (c + dc) % NC, (z + dz) % NZ, y))
+    for peer in peers:
+        pl.semaphore_signal(barrier, inc=1, device_id=peer, device_id_type=MESH_ID)
+    pl.semaphore_wait(barrier, len(peers))
+
+
+def remote(src, dst, sems, peer):
+    return pltpu.make_async_remote_copy(
+        src_ref=src,
+        dst_ref=dst,
+        send_sem=sems.take(),
+        recv_sem=sems.take(),
+        device_id=peer,
+        device_id_type=MESH_ID,
+    )
+
+
+class Gather:
+    def __init__(self, kind, src, dst, sems):
+        self.kind, self.src, self.dst = kind, src, dst
+        x, c, z, y = place()
+        self.first = []
+        if kind == "row":
+            here = dst.at[x, z, y]
+            self.local = pltpu.make_async_copy(src, here, sems.take())
+            for dz in range(1, NZ):
+                self.first.append(remote(src, here, sems, (x, c, (z + dz) % NZ, y)))
+            mine = dst.at[x, :, y]
+            via_y = dst.at[1 - x, 0:2, y]
+            via_x = dst.at[x, 2:4, 1 - y]
+        else:
+            here = dst.at[x, c, z, y]
+            pick = (lambda core: src.at[core]) if kind == "col" else (lambda core: src)
+            self.local = pltpu.make_async_copy(pick(c), here, sems.take())
+            for dz in range(NZ):
+                for dc in range(NC):
+                    if dz or dc:
+                        core = (c + dc) % NC
+                        self.first.append(remote(pick(core), here, sems, (x, core, (z + dz) % NZ, y)))
+            mine = dst.at[x, :, :, y]
+            via_y = dst.at[1 - x, 0, :, y]
+            via_x = dst.at[x, 1, :, 1 - y]
+        self.second = [
+            remote(mine, mine, sems, (1 - x, c, z, y)),
+            remote(mine, mine, sems, (x, c, z, 1 - y)),
+        ]
+        self.third = [
+            remote(via_y, via_y, sems, (x, c, z, 1 - y)),
+            remote(via_x, via_x, sems, (1 - x, c, z, y)),
+        ]
+
+    def start_first(self):
+        self.local.start()
+        for item in self.first:
+            item.start()
+
+    def start_second(self):
+        self.local.wait()
+        for item in self.first:
+            item.wait_recv()
+        for item in self.second:
+            item.start()
+
+    def start_third(self):
+        for item in self.second:
+            item.wait_recv()
+        for item in self.third:
+            item.start()
+
+    def finish(self):
+        for item in self.third:
+            item.wait_recv()
+        for item in self.first + self.second + self.third:
+            item.wait_send()
+
+
+class Rows:
+    def __init__(self, src, own, other, sems):
+        x, c, z, y = place()
+        self.other = other
+        self.relay = c == z // 2
+        self.go, self.stay = [], []
+        send = [sems.take(), sems.take()]
+        recv = [sems.take() for _ in range(NZ)]
+        local = sems.take()
+        base = sems.used - NZ - 1
+        for i in range(2):
+            self.go.append(
+                pltpu.make_async_remote_copy(
+                    src_ref=src.at[i],
+                    dst_ref=own.at[z],
+                    send_sem=send[i],
+                    recv_sem=sems.ref.at[base + z],
+                    device_id=(x, c, 2 * c + i, y),
+                    device_id_type=MESH_ID,
+                )
+            )
+            self.stay.append(pltpu.make_async_copy(src.at[i], own.at[z], local))
+        self.arrive = []
+        for dz in range(1, NZ):
+            zs = (z + dz) % NZ
+            self.arrive.append(
+                pltpu.make_async_remote_copy(
+                    src_ref=src.at[0],
+                    dst_ref=own.at[zs],
+                    send_sem=send[0],
+                    recv_sem=sems.ref.at[base + zs],
+                    device_id=(x, c, zs, y),
+                    device_id_type=MESH_ID,
+                )
+            )
+        self.pass_own = remote(own, own, sems, (x, 1 - c, z, y))
+        if other is not None:
+            self.cross = remote(own, other, sems, (x, c, z, 1 - y))
+            self.pass_other = remote(other, other, sems, (x, 1 - c, z, y))
+
+    def start(self):
+        x, c, z, y = place()
+        for i in range(2):
+            @pl.when(2 * c + i != z)
+            def _():
+                self.go[i].start()
+
+            @pl.when(2 * c + i == z)
+            def _():
+                self.stay[i].start()
+
+    def forward(self):
+        @pl.when(self.relay)
+        def _():
+            self.stay[0].wait()
+            for item in self.arrive:
+                item.wait_recv()
+            if self.other is not None:
+                self.cross.start()
+            self.pass_own.start()
+
+    def forward_other(self):
+        if self.other is not None:
+            @pl.when(self.relay)
+            def _():
+                self.cross.wait_recv()
+                self.pass_other.start()
+
+    def finish(self):
+        x, c, z, y = place()
+        for i in range(2):
+            @pl.when(2 * c + i != z)
+            def _():
+                self.go[i].wait_send()
+
+        @pl.when(self.relay)
+        def _():
+            self.pass_own.wait_send()
+            if self.other is not None:
+                self.cross.wait_send()
+                self.pass_other.wait_send()
+
+        @pl.when(jnp.logical_not(self.relay))
+        def _():
+            self.pass_own.wait_recv()
+            if self.other is not None:
+                self.pass_other.wait_recv()
+
+
+def gather_kernel(qkv, w_in, w_out, w_down, small, tokens, cotangent,
+                  qkv0, qkv1, in0, in1, out0, out1, down0, down1, smalls, own, other, back,
+                  sem_ref):
+    sems = Sems(sem_ref)
+    rows = Rows(tokens, own, other, sems)
+    back_rows = Rows(cotangent, back, None, sems)
+    items = [
+        Gather("col", qkv.at[0], qkv0, sems),
+        Gather("both", small, smalls, sems),
+        Gather("row", w_out.at[0], out0, sems),
+        Gather("col", w_in.at[0], in0, sems),
+        Gather("row", w_down.at[0], down0, sems),
+        Gather("col", qkv.at[1], qkv1, sems),
+        Gather("row", w_out.at[1], out1, sems),
+        Gather("col", w_in.at[1], in1, sems),
+        Gather("row", w_down.at[1], down1, sems),
+    ]
+    enter_barrier()
+    rows.start()
+    for item in items:
+        item.start_first()
+    back_rows.start()
+    count = len(items)
+    for step in range(count + 1):
+        if step < count:
+            items[step].start_second()
+        if step == 0:
+            rows.forward()
+        if step >= 1:
+            items[step - 1].start_third()
+        if step == 2:
+            rows.forward_other()
+    back_rows.forward()
+    for item in items:
+        item.finish()
+    rows.finish()
+    back_rows.finish()
+
+
+GATHER_SEMS = 260
+
+
+def gather_all(qkv, w_in, w_out, w_down, small, tokens, cotangent):
+    hbm = pl.BlockSpec(memory_space=pl.ANY)
+    shapes = [
+        (2, 2, 4, 2, 24, 1152), (2, 2, 4, 2, 24, 1152),
+        (2, 2, 4, 2, 24, 1536), (2, 2, 4, 2, 24, 1536),
+        (2, 4, 2, 24, 768), (2, 4, 2, 24, 768),
+        (2, 4, 2, 96, 768), (2, 4, 2, 96, 768),
+        (2, 2, 4, 2, 8, 128),
+        (4, 128, 768), (4, 128, 768), (4, 128, 768),
+    ]
+    return pl.pallas_call(
+        gather_kernel,
+        out_shape=[jax.ShapeDtypeStruct(s, BF16) for s in shapes],
+        in_specs=[hbm] * 7,
+        out_specs=[hbm] * len(shapes),
+        scratch_shapes=[pltpu.SemaphoreType.DMA((GATHER_SEMS,))],
+        compiler_params=pltpu.CompilerParams(collective_id=0, has_side_effects=True),
+        name="gather_all",
+    )(qkv, w_in, w_out, w_down, small, tokens, cotangent)
+
+
+class Reduce:
+    def __init__(self, kind, part, sems, first, second, third, out):
+        x, c, z, y = place()
+        self.kind, self.part, self.out = kind, part, out
+        self.first_buf, self.second_buf, self.third_buf = first, second, third
+        if kind == "row":
+            via_y, via_x = part.at[1 - x, 0:2, 1 - y], part.at[1 - x, 2:4, 1 - y]
+            to_x, to_y = part.at[1 - x, :, y], part.at[x, :, 1 - y]
+        else:
+            via_y, via_x = part.at[1 - x, 0, :, 1 - y], part.at[1 - x, 1, :, 1 - y]
+            to_x, to_y = part.at[1 - x, :, :, y], part.at[x, :, :, 1 - y]
+        self.first = [
+            remote(via_y, first.at[0], sems, (x, c, z, 1 - y)),
+            remote(via_x, first.at[1], sems, (1 - x, c, z, y)),
+        ]
+        self.second = [
+            remote(to_x, second.at[0], sems, (1 - x, c, z, y)),
+            remote(to_y, second.at[1], sems, (x, c, z, 1 - y)),
+        ]
+        self.third = []
+        if kind == "row":
+            for dz in range(1, NZ):
+                zt = (z + dz) % NZ
+                self.third.append(remote(part.at[x, zt, y], third.at[z], sems, (x, c, zt, y)))
+            self.local = pltpu.make_async_copy(part.at[x, z, y], third.at[z], sems.take())
+        else:
+            for dz in range(NZ):
+                for dc in range(NC):
+                    if dz or dc:
+                        zt, core = (z + dz) % NZ, (c + dc) % NC
+                        self.third.append(
+                            remote(part.at[x, core, zt, y], third.at[z, c], sems, (x, core, zt, y))
+                        )
+            self.local = pltpu.make_async_copy(part.at[x, c, z, y], third.at[z, c], sems.take())
+
+    def start_first(self):
+        for item in self.first:
+            item.start()
+
+    def start_second(self):
+        x, c, z, y = place()
+        part, first = self.part, self.first_buf
+        for item in self.first:
+            item.wait_recv()
+        if self.kind == "row":
+            def add(k, carry):
+                part[1 - x, k, y] = (part[1 - x, k, y].astype(F32) + first[0, k].astype(F32)).astype(BF16)
+                part[x, 2 + k, 1 - y] = (part[x, 2 + k, 1 - y].astype(F32) + first[1, k].astype(F32)).astype(BF16)
+                return carry
+            lax.fori_loop(0, 2, add, 0)
+        else:
+            def add(k, carry):
+                part[1 - x, 0, k, y] = (part[1 - x, 0, k, y].astype(F32) + first[0, k].astype(F32)).astype(BF16)
+                part[x, 1, k, 1 - y] = (part[x, 1, k, 1 - y].astype(F32) + first[1, k].astype(F32)).astype(BF16)
+                return carry
+            lax.fori_loop(0, 4, add, 0)
+        for item in self.second:
+            item.start()
+
+    def start_third(self):
+        x, c, z, y = place()
+        part, second = self.part, self.second_buf
+        for item in self.second:
+            item.wait_recv()
+        if self.kind == "row":
+            def add(k, carry):
+                part[x, k, y] = (
+                    part[x, k, y].astype(F32) + second[0, k].astype(F32) + second[1, k].astype(F32)
+                ).astype(BF16)
+                return carry
+            lax.fori_loop(0, 4, add, 0)
+        else:
+            def add(k, carry):
+                h, j = k // 4, k % 4
+                part[x, h, j, y] = (
+                    part[x, h, j, y].astype(F32) + second[0, h, j].astype(F32) + second[1, h, j].astype(F32)
+                ).astype(BF16)
+                return carry
+            lax.fori_loop(0, 8, add, 0)
+        self.local.start()
+        for item in self.third:
+            item.start()
+
+    def finish(self):
+        self.local.wait()
+        for item in self.third:
+            item.wait_recv()
+        third, out = self.third_buf, self.out
+        if self.kind == "row":
+            out[...] = (
+                third[0].astype(F32) + third[1].astype(F32) + third[2].astype(F32) + third[3].astype(F32)
+            )
+        else:
+            for h in range(NC):
+                out[h] = (
+                    third[0, h].astype(F32) + third[1, h].astype(F32)
+                    + third[2, h].astype(F32) + third[3, h].astype(F32)
+                )
+        for item in self.first + self.second + self.third:
+            item.wait_send()
+
+
+class Home:
+    def __init__(self, own, dst, sems):
+        x, c, z, y = place()
+        self.relay = c == z // 2
+        base = sems.used
+        for _ in range(2 * NZ + 3):
+            sems.take()
+        self.go = []
+        for dz in range(1, NZ):
+            zt = (z + dz) % NZ
+            self.go.append(
+                pltpu.make_async_remote_copy(
+                    src_ref=own.at[zt],
+                    dst_ref=dst.at[z % 2],
+                    send_sem=sems.ref.at[base + dz],
+                    recv_sem=sems.ref.at[base + NZ + z % 2],
+                    device_id=(x, c, zt, y),
+                    device_id_type=MESH_ID,
+                )
+            )
+        self.stay = pltpu.make_async_copy(own.at[z], dst.at[z % 2], sems.ref.at[base])
+        self.arrive = []
+        for i in range(2):
+            self.arrive.append(
+                pltpu.make_async_remote_copy(
+                    src_ref=own.at[0],
+                    dst_ref=dst.at[i],
+                    send_sem=sems.ref.at[base + 1],
+                    recv_sem=sems.ref.at[base + NZ + i],
+                    device_id=(x, c, z, 1 - y),
+                    device_id_type=MESH_ID,
+                )
+            )
+
+    def start(self):
+        @pl.when(self.relay)
+        def _():
+            self.stay.start()
+            for item in self.go:
+                item.start()
+
+    def finish(self):
+        x, c, z, y = place()
+
+        @pl.when(self.relay)
+        def _():
+            self.stay.wait()
+            for item in self.go:
+                item.wait_send()
+
+        for i in range(2):
+            @pl.when(2 * c + i != z)
+            def _():
+                self.arrive[i].wait_recv()
+
+
+KINDS = ("col", "col", "row", "row", "row")
+PART_SHAPES = (
+    (2, 2, 4, 2, 24, 1152), (2, 2, 4, 2, 24, 1536), (2, 4, 2, 24, 768), (2, 4, 2, 96, 768), (2, 4, 2, 8, 128),
+)
+
+
+def reduce_buffers(kind, shape):
+    block = shape[-2:]
+    if kind == "row":
+        return [(2, 2) + block, (2, 4) + block, (4,) + block]
+    return [(2, 4) + block, (2, 2, 4) + block, (4, 2) + block]
+
+
+def owner_shape(kind, shape):
+    return shape[-2:] if kind == "row" else (2,) + shape[-2:]
+
+
+def reduce_kernel(kinds, *refs):
+    count = len(kinds)
+    parts = refs[:count]
+    out_rows, back_rows = refs[count:count + 2]
+    outs = refs[count + 2:2 * count + 2]
+    out_home, back_home = refs[2 * count + 2:2 * count + 4]
+    buffers = refs[2 * count + 4:-1]
+    sems = Sems(refs[-1])
+    items = [
+        Reduce(kinds[k], parts[k], sems, *buffers[3 * k:3 * k + 3], outs[k]) for k in range(count)
+    ]
+    homes = [Home(back_rows, back_home, sems), Home(out_rows, out_home, sems)]
+    enter_barrier()
+    for item in items:
+        item.start_first()
+    for home in homes:
+        home.start()
+    for step in range(count + 1):
+        if step < count:
+            items[step].start_second()
+        if step >= 1:
+            items[step - 1].start_third()
+    for item in items:
+        item.finish()
+    for home in homes:
+        home.finish()
+
+
+def reduce_all(kinds, parts, out_rows, back_rows):
+    vmem = pl.BlockSpec(memory_space=pltpu.VMEM)
+    hbm = pl.BlockSpec(memory_space=pl.ANY)
+    count = len(kinds)
+    scratch = []
+    for kind, part in zip(kinds, parts):
+        for shape in reduce_buffers(kind, part.shape):
+            scratch.append(pltpu.VMEM(shape, BF16))
+    scratch.append(pltpu.SemaphoreType.DMA((GATHER_SEMS,)))
+    out_shape = [jax.ShapeDtypeStruct(owner_shape(k, p.shape), F32) for k, p in zip(kinds, parts)]
+    out_shape += [jax.ShapeDtypeStruct((2, 128, 768), BF16)] * 2
+    return pl.pallas_call(
+        partial(reduce_kernel, kinds),
+        out_shape=out_shape,
+        in_specs=[vmem] * count + [hbm] * 2,
+        out_specs=[vmem] * count + [hbm] * 2,
+        scratch_shapes=scratch,
+        compiler_params=pltpu.CompilerParams(
+            collective_id=1, has_side_effects=True, vmem_limit_bytes=60 * 1024 * 1024
+        ),
+        name="reduce_all",
+    )(*parts, out_rows, back_rows)
+
+
+def swap(value, axis):
+    return lax.ppermute(value, axis, [(0, 1), (1, 0)])
+
+
+def core_sum(value):
+    mine = value.astype(BF16)
+    other = swap(mine, "c")
+    return mine.astype(F32) + other.astype(F32)
+
+
+def layer_forward(hidden, inputs, weights, key_mask):
+    qkv, w_in, w_out, w_down, params = weights
+    b_query, b_value, b_in, b_out, b_down, gain_one, shift_one, gain_two, shift_two = params
+    rows = hidden.shape[0]
+    query = (dot_plain(inputs[:rows], qkv[:, :384]) + b_query).astype(BF16)
+    key = dot_plain(inputs, qkv[:, 384:768]).astype(BF16)
+    value = (dot_plain(inputs, qkv[:, 768:]) + b_value).astype(BF16)
+    q3, k3, v3 = (t.reshape(-1, 6, 64).transpose(1, 0, 2) for t in (query, key, value))
+    scores = jnp.einsum("hqd,hkd->hqk", q3, k3, preferred_element_type=F32) * 0.125
+    scores = jnp.where(key_mask[None, None, :], scores, NEG)
+    log_norm = jax.nn.logsumexp(scores, axis=-1, keepdims=True)
+    probs = jnp.exp(scores - log_norm).astype(BF16)
+    context = jnp.einsum("hqk,hkd->qhd", probs, v3, preferred_element_type=F32).astype(BF16).reshape(rows, 384)
+    first = hidden + core_sum(dot_plain(context, w_out)) + b_out
+    normed_one, hat_one, spread_one = layer_norm(first, gain_one, shift_one)
+    ff_in = normed_one.astype(BF16)
+    pre_act = dot_plain(ff_in, w_in) + b_in
+    activated = jax.nn.gelu(pre_act, approximate=False).astype(BF16)
+    second = normed_one + core_sum(dot_plain(activated, w_down)) + b_down
+    result, hat_two, spread_two = layer_norm(second, gain_two, shift_two)
+    kept = (inputs, q3, k3, v3, log_norm, context, hat_one, spread_one, ff_in, pre_act, activated, hat_two, spread_two)
+    return result, kept
+
+
+def layer_backward(back, kept, weights, key_mask):
+    qkv, w_in, w_out, w_down, params = weights
+    b_query, b_value, b_in, b_out, b_down, gain_one, shift_one, gain_two, shift_two = params
+    inputs, q3, k3, v3, log_norm, context, hat_one, spread_one, ff_in, pre_act, activated, hat_two, spread_two = kept
+    rows = back.shape[0]
+    back_second, g_gain_two, g_shift_two = norm_back(back, hat_two, spread_two, gain_two)
+    back_down = back_second.astype(BF16)
+    g_down = dot_left_t(activated, back_down)
+    g_b_down = jnp.sum(back_down.astype(F32), 0)
+    back_act = dot_right_t(back_down, w_down)
+    gelu_pull = jax.vjp(partial(jax.nn.gelu, approximate=False), pre_act)[1]
+    back_pre = gelu_pull(back_act)[0].astype(BF16)
+    g_in = dot_left_t(ff_in, back_pre)
+    g_b_in = jnp.sum(back_pre.astype(F32), 0)
+    back_normed = back_second + core_sum(dot_right_t(back_pre, w_in))
+    back_first, g_gain_one, g_shift_one = norm_back(back_normed, hat_one, spread_one, gain_one)
+    back_branch = back_first.astype(BF16)
+    g_out = dot_left_t(context, back_branch)
+    g_b_out = jnp.sum(back_branch.astype(F32), 0)
+    back_context = dot_right_t(back_branch, w_out).astype(BF16)
+    b3 = back_context.reshape(rows, 6, 64).transpose(1, 0, 2)
+    scores = jnp.einsum("hqd,hkd->hqk", q3, k3, preferred_element_type=F32) * 0.125
+    scores = jnp.where(key_mask[None, None, :], scores, NEG)
+    probs = jnp.exp(scores - log_norm)
+    slope = jnp.einsum("hqd,hkd->hqk", b3, v3, preferred_element_type=F32)
+    delta = jnp.sum(probs * slope, -1, keepdims=True)
+    score_back = (probs * (slope - delta)).astype(BF16)
+    back_value = jnp.einsum("hqk,hqd->khd", probs.astype(BF16), b3, preferred_element_type=F32)
+    back_query = jnp.einsum("hqk,hkd->qhd", score_back, k3, preferred_element_type=F32) * 0.125
+    back_key = jnp.einsum("hqk,hqd->khd", score_back, q3, preferred_element_type=F32) * 0.125
+    back_query = back_query.astype(BF16).reshape(rows, 384)
+    back_key = back_key.astype(BF16).reshape(2 * rows, 384)
+    back_value = back_value.astype(BF16).reshape(2 * rows, 384)
+    g_qkv = jnp.concatenate(
+        [dot_left_t(inputs[:rows], back_query), dot_left_t(inputs, back_key), dot_left_t(inputs, back_value)], 1
+    )
+    g_b_query = jnp.sum(back_query.astype(F32), 0)
+    g_b_value = jnp.sum(back_value.astype(F32), 0)
+    both = dot_right_t(back_key, qkv[:, 384:768]) + dot_right_t(back_value, qkv[:, 768:])
+    mine = both[:rows] + dot_right_t(back_query, qkv[:, :384])
+    other = core_sum(both[rows:]).astype(BF16)
+    result = back_first + core_sum(mine) + swap(other, "y").astype(F32)
+    grads = (g_qkv, g_in, g_out, g_down)
+    small = (g_b_query, g_b_value, g_b_in, g_b_out, g_b_down, g_gain_one, g_shift_one, g_gain_two, g_shift_two)
+    return result, grads, small
+
+
+def pick_core(value, core, width):
+    both = value.reshape(2, 2, 4 * 2 * width)
+    return lax.dynamic_index_in_dim(both, core, 1, keepdims=False).reshape(2, 4, 2, width)
+
+
+def chip_device(tokens, lengths, slot_sequence, cotangent, w_query, w_key, w_value, w_out, w_in, w_down,
+                b_query, b_value, b_out, b_in, b_down, norm1_gain, norm1_bias, norm2_gain, norm2_bias):
+    x, c, z, y = place()
+    slot = 4 * x + z
+    sequence = jnp.sum(jnp.where(lax.iota(jnp.int32, 8) == slot, slot_sequence, 0))
+    length = jnp.sum(jnp.where(lax.iota(jnp.int32, 8) == sequence, lengths, 0))
+    ids = lax.iota(jnp.int32, 512)
+    spot = 256 * (ids // 128) + ids % 128
+    own_pos, other_pos = spot + 128 * y, spot + 128 * (1 - y)
+    key_mask = jnp.concatenate([own_pos, other_pos]) < length
+    row_valid = (own_pos < length)[:, None]
+
+    qkv = jnp.stack([w_query, w_key, w_value]).reshape(3, 2, 24, 2, 2, 192)
+    qkv = qkv.transpose(1, 4, 2, 0, 3, 5).reshape(2, 2, 24, 1152)
+    win = w_in.reshape(2, 24, 2, 2, 768).transpose(0, 3, 1, 2, 4).reshape(2, 2, 24, 1536)
+    small = jnp.concatenate(
+        [b_query, b_value, b_out, b_down, norm1_gain, norm1_bias, norm2_gain, norm2_bias, b_in,
+         jnp.zeros((2, 224), BF16)], 1).reshape(8, 128)
+    (qkv0, qkv1, in0, in1, out0, out1, down0, down1, smalls, own, other, back) = gather_all(
+        qkv, win, w_out, w_down, small, tokens, cotangent)
+    table = smalls.reshape(32, 2, 512)[:, :, :288].astype(F32)
+    wide = table[:, :, :192].reshape(32, 2, 8, 24).transpose(1, 2, 0, 3).reshape(2, 8, 768)
+    tall = table[:, :, 192:].transpose(1, 0, 2).reshape(2, 3072)
+
+    def half(vector, width):
+        return lax.dynamic_index_in_dim(vector.reshape(2, 2, width), c, 1, keepdims=False).reshape(2 * width)
+
+    weights = []
+    for layer, group in enumerate(((qkv0, in0, out0, down0), (qkv1, in1, out1, down1))):
+        bq, bv, bo, bd, g1, s1, g2, s2 = (wide[layer, k] for k in range(8))
+        params = (half(bq, 192), half(bv, 192), half(tall[layer], 768), bo, bd, g1, s1, g2, s2)
+        weights.append((group[0].reshape(768, 1152), group[1].reshape(768, 1536),
+                        group[2].reshape(384, 768), group[3].reshape(1536, 768), params))
+
+    own = own.reshape(512, 768)
+    other = other.reshape(512, 768)
+    hidden = own.astype(F32)
+    inputs = jnp.concatenate([own, other], 0)
+    kept = []
+    for layer in range(2):
+        hidden, saved = layer_forward(hidden, inputs, weights[layer], key_mask)
+        kept.append(saved)
+        if layer == 0:
+            mine = hidden.astype(BF16)
+            inputs = jnp.concatenate([mine, swap(mine, "y")], 0)
+    back = jnp.where(row_valid, back.reshape(512, 768).astype(F32), 0.0)
+    parts, smalls = [None] * 2, [None] * 2
+    for layer in (1, 0):
+        back, grads, small = layer_backward(back, kept[layer], weights[layer], key_mask)
+        g_qkv, g_in, g_out, g_down = grads
+        parts[layer] = [g_qkv.astype(BF16).reshape(PART_SHAPES[0]), g_in.astype(BF16).reshape(PART_SHAPES[1]),
+                        g_out.astype(BF16).reshape(PART_SHAPES[2]), g_down.astype(BF16).reshape(PART_SHAPES[3])]
+        bq, bv, bi, bo, bd, g1, s1, g2, s2 = small
+        pieces = [bq.reshape(2, 4, 2, 24), bv.reshape(2, 4, 2, 24)]
+        pieces += [pick_core(v, c, 24) for v in (bo, bd, g1, s1, g2, s2)]
+        pieces += [bi.reshape(2, 4, 2, 96), jnp.zeros((2, 4, 2, 224), F32)]
+        smalls[layer] = jnp.concatenate(pieces, -1)
+    small_part = jnp.concatenate(smalls, -1).reshape(2, 4, 2, 8, 128).astype(BF16)
+    kinds = KINDS[:4] + KINDS
+    out = reduce_all(kinds, parts[1] + parts[0] + [small_part],
+                     hidden.astype(BF16).reshape(4, 128, 768), back.astype(BF16).reshape(4, 128, 768))
+    qkv_out = jnp.stack([out[4], out[0]]).reshape(2, 2, 24, 3, 2, 192)
+    qkv_out = qkv_out.transpose(3, 0, 2, 4, 1, 5).reshape(3, 2, 24, 768)
+    in_out = jnp.stack([out[5], out[1]]).reshape(2, 2, 24, 2, 768).transpose(0, 2, 3, 1, 4).reshape(2, 24, 3072)
+    vec = out[8].reshape(2, 512)
+    vecs = [vec[:, 24 * k:24 * k + 24] for k in range(8)]
+    return (out[9].astype(F32), out[10].astype(F32), qkv_out[0], qkv_out[1], qkv_out[2],
+            jnp.stack([out[6], out[2]]), in_out, jnp.stack([out[7], out[3]]),
+            vecs[0], vecs[1], vecs[2], vec[:, 192:288], vecs[3], vecs[4], vecs[5], vecs[6], vecs[7])
+
+
+def solution(mesh):
+    if dict(mesh.shape) != {"head": 4, "blk": 8}:
+        return plain_solution(mesh)
+    grid = Mesh(mesh.devices.reshape(NX, NC, NZ, NY), AXES)
+    rows = P(("x", "c"), ("z", "y"), None)
+    wide = P(None, AXES, None)
+    flat = P(None, AXES)
+    return jax.shard_map(
+        chip_device,
+        mesh=grid,
+        in_specs=(rows, P(), P(), rows) + (wide,) * 6 + (flat,) * 9,
+        out_specs=(rows, rows) + (wide,) * 6 + (flat,) * 9,
+        check_vma=False,
+    )

time: 2400 us -> 630 us (0.26)
  waiting for transfers between devices: 1530 us -> 52 us
  Pallas kernels: 0 us -> 315 us
  blocking collectives: 205 us -> 0 us
  matrix products: 306 us -> 120 us
  local copies, waits for them, and re-layouts: 229 us -> 61.8 us
  starting transfers between devices: 30.8 us -> 3.5 us
    unnamed x22 -> x0, waiting for transfers between devices: 809 us -> none
    all_gather x20 -> x0, waiting for transfers between devices: 717 us -> none  [the longest x2 128 us: fetch_forward(): lax.all_gather(shards[4][layer_index], ('head', 'blk'), axis=0, tiled=True)]
    pallas_call x0 -> x2, Pallas kernels: none -> 315 us  [the longest x1 167 us: gather_all(): pl.pallas_call(gather_kernel, out_shape=[jax.ShapeDtypeStruct(s, BF16) fo...]
    dot_general x36 -> x12, matrix products: 200 us -> 41 us  [the longest x2 12.8 us: layer_backward(): slope = jnp.einsum('hqd,hkd->hqk', b3, v3, preferred_element_type=F32)]
    all_gather x4 -> x0, blocking collectives: 115 us -> none  [the longest x2 59.1 us: attention_backward(): lax.all_gather(log_norm, 'blk', axis=1, tiled=True)]
    unnamed x333 -> x240, local copies, waits for them, and re-layouts: 96.2 us -> 9.24 us
    reshape x34 -> x40, local copies, waits for them, and re-layouts: 75.9 us -> 17.5 us  [the longest x12 4.84 us: pick_core(): lax.dynamic_index_in_dim(both, core, 1, keepdims=False)]
    ppermute x0 -> x13, waiting for transfers between devices: none -> 52 us  [swap(): return lax.ppermute(value, axis, [(0, 1), (1, 0)])]
  transfers between devices with their start and end apart: 26 -> 13, of which waited for: 18 -> 5; matrix products, arithmetic and copies ran while one was open for 19% -> 13% of each run, Pallas kernels for 0% -> 0%
where the time goes in v1:
time: 630 us; the launch traced here: 623 us
  Pallas kernels  315 us (50%)
  matrix products  120 us (19%)
  other arithmetic  68.3 us (11%)
  local copies, waits for them, and re-layouts  61.8 us (10%)
  waiting for transfers between devices  52 us (8%)
    pallas_call x1, Pallas kernels, gather_all(): pl.pallas_call(gather_kernel, out_shape=[jax.ShapeDtypeStruct(s, BF16) fo...  167 us
    pallas_call x1, Pallas kernels, reduce_all(): pl.pallas_call(partial(reduce_kernel, kinds), out_shape=out_shape, in_spe...  148 us
    ppermute x13, waiting for transfers between devices, swap(): return lax.ppermute(value, axis, [(0, 1), (1, 0)])  52 us
    dot_general x12, matrix products, dot_plain(): return jnp.dot(former, latter, preferred_element_type=jnp.float32)  38.7 us
    dot_general x12, matrix products, dot_left_t(): lax.dot_general(former, latter, (((0,), (0,)), ((), ())), preferred_eleme...  23.1 us
    dot_general x12, matrix products, dot_right_t(): lax.dot_general(former, latter, (((1,), (1,)), ((), ())), preferred_eleme...  17.1 us
    convert_element_type x2, other arithmetic, layer_backward(): score_back = (probs * (slope - delta)).astype(BF16)  14.1 us
    dot_general x2, matrix products, layer_backward(): slope = jnp.einsum('hqd,hkd->hqk', b3, v3, preferred_element_type=F32)  12.8 us
  transfers between devices with their start and end apart: 13, of which 5 were waited for; matrix products, arithmetic and copies ran while one was open for 13% of the time, Pallas kernels for 0%

profile of v1, /device:TPU:0, one launch (start us, length us, event | category | flops | bytes accessed | tf_op | source)
XLA Modules:
  0.0 623.3 jit_solution(4535151074000649836)
XLA Ops:
  7.7 166.9 %gather_all.1 = (bf16[2,2,4,2,24,1152]{5,4,3,2,1,0:T(8,128)(2,1)}, bf16[2,2,4,2,24,1152]{5,4,3,2,1,0:T(8,128)(2,1)}, bf16[2,2,4,2,24,1536]{5,4,3,2,1,0:T(8,128)(...) custom-call(bf16[2,2,24,1152]{3,2,1,0:T(8,128)(2,1)} %reshape.539.qk, ...), custom_call_target="tpu_custom_call" | custom-call | tf_op jit(solution)/shard_map/gather_all/pallas_call | solution.py:796
  178.9 2.0 convolution_convert_fusion.5
  183.6 1.9 fusion
  185.6 3.2 exponential_reduce_fusion.1
  190.3 1.9 add_convert_fusion.7
  192.2 7.5 %convolution_convert_fusion.25 = bf16[6,64,512]{2,1,0:T(8,128)(2,1)S(1)} fusion(bf16[6,1024,64]{1,2,0:T(8,128)(2,1)S(1)} %bitcast.260, f32[6,512,1024]{2,1,0:T(8,128)} %copy-done, f32[6,512]{1,0:T(8,128)S(1)} %log_add_fusion.1, pred[1024]{0:T(1024)(128)(4,1)S(1)} %add_compare_fusion), kind=kOutput, calls=%fused_computation.148 | convolution fusion | flops 415432704 | bytes 13775872 | tf_op jit(solution)/shard_map/hqk,hkd->qhd/dot_general | solution.py:1056
  205.7 9.9 %multiply_convert_fusion.3 = (bf16[512,1536]{1,0:T(8,128)(2,1)S(1)}, f32[512,1536]{1,0:T(8,128)}, f32[512,1536]{1,0:T(8,128)}) fusion(f32[1536]{0:T(1024)S(1)} %add.383, bf16[768,1536]{1,0:T(8,128)(2,1)S(1)} %bitcast.275, f32[512,768]{1,0:T(8,128)S(1)} %get-tuple-element.117, f32[768]{0:T(1024)S(1)} %get-tuple-element.90, f32[768]{0:T(1024)S(1)} %get-tuple-element.91, ...), kind=kOutput, calls=%fused_computation.39 | convolution fusion | flops 1261830144 | bytes 11812864 | tf_op jit(solution)/shard_map/dot_general | solution.py:21
  217.2 2.2 collective-permute-done.1
  225.5 16.1 %collective-permute-done.2 = bf16[512,768]{1,0:T(8,128)(2,1)} collective-permute-done((bf16[512,768]{1,0:T(8,128)(2,1)}, bf16[512,768]{1,0:T(8,128)(2,1)}, u32[]{:S(2)}, u32[]{:S(2)}) %collective-permute-start.2) | collective-permute-done | bytes 786464 | tf_op jit(solution)/shard_map/ppermute | solution.py:1035
  241.6 2.4 convolution_convert_fusion.4
  243.9 1.9 fusion.1
  245.9 2.9 exponential_reduce_fusion
  248.9 3.6 add_convert_fusion.6
  252.6 3.0 convolution_convert_fusion.24
  261.9 2.2 fusion.127
  264.5 9.5 %multiply_convert_fusion.2 = (bf16[512,1536]{1,0:T(8,128)(2,1)S(1)}, f32[512,1536]{1,0:T(8,128)}, f32[512,1536]{1,0:T(8,128)}) fusion(f32[1536]{0:T(1024)S(1)} %copy-done.81, bf16[768,1536]{1,0:T(8,128)(2,1)S(1)} %bitcast.279, f32[512,768]{1,0:T(8,128)S(1)} %get-tuple-element.111, f32[768]{0:T(1024)S(1)} %copy-done.75, f32[768]{0:T(1024)S(1)} %copy-done.57, ...), kind=kOutput, calls=%fused_computation.26 | convolution fusion | flops 1261830144 | bytes 11812864 | tf_op jit(solution)/shard_map/dot_general | solution.py:21
  274.1 2.3 convolution_convert_fusion.10
  281.8 2.3 copy.87
  284.1 2.6 fusion.42
  286.7 2.6 copy.89
  291.8 1.9 fusion.200
  293.6 2.3 copy.82
  296.0 2.6 fusion.125
  300.2 2.2 convert_reduce_fusion
  302.7 2.9 fusion.135
  305.5 2.3 convolution_convert_fusion.9
  307.9 2.6 fusion.41
  310.5 2.8 copy.84
  322.7 4.8 convolution_convert_fusion.2
  327.6 3.0 convolution_convert_fusion.3
  330.6 3.5 multiply_reduce_fusion.3
  336.3 6.4 %multiply_reduce_fusion.1 = (f32[6,512]{1,0:T(8,128)S(1)}, f32[6,512,1024]{2,1,0:T(8,128)}) fusion(f32[6,512,1024]{2,1,0:T(8,128)S(1)} %bitcast.198, f32[6,512]{1,0:T(8,128)S(1)} %copy-done.50, pred[1024]{0:T(1024)(128)(4,1)S(1)} %add_compare_fusion, bf16[6,512,64]{1,2,0:T(8,128)(2,1)S(1)} %bitcast.254, bf16[6,1024,64]{1,2,0:T(8,128)(2,1)S(1)} %bitcast.263), kind=kOutput, calls=%fused_computation.3 | convolution fusion | flops 418378752 | bytes 26371072 | tf_op jit(solution)/shard_map/hqd,hkd->hqk/dot_general | solution.py:1092
  342.6 3.9 bitcast_reduce_fusion.1
  346.5 7.0 %multiply_convert_fusion.1 = bf16[6,512,1024]{2,1,0:T(8,128)(2,1)S(1)} fusion(f32[6,512,1024]{2,1,0:T(8,128)} %get-tuple-element.139, f32[6,512,1024]{2,1,0:T(8,128)S(1)} %bitcast.198, f32[6,512]{1,0:T(8,128)S(1)} %get-tuple-element.138, f32[6,512]{1,0:T(8,128)S(1)} %copy-done.50, pred[1024]{0:T(1024)(128)(4,1)S(1)} %add_compare_fusion), kind=kLoop, calls=%fused_computation.2 | loop fusion | flops 18874368 | bytes 31482880 | tf_op jit(solution)/shard_map/convert_element_type | solution.py:1094
  357.7 2.1 bitcast_reduce_fusion.3
  366.0 15.9 %collective-permute-done.8 = bf16[512,768]{1,0:T(8,128)(2,1)S(1)} collective-permute-done((bf16[512,768]{1,0:T(8,128)(2,1)S(1)}, bf16[512,768]{1,0:T(8,128)(2,1)S(1)}, u32[]{:S(2)}, u32[]{:S(2)}) %collective-permute-start.8) | collective-permute-done | bytes 786464 | tf_op jit(solution)/shard_map/ppermute | solution.py:1035
  386.2 2.3 fusion.134
  389.7 2.5 convolution_convert_fusion.7
  395.2 4.4 convolution_convert_fusion
  399.6 3.0 convolution_convert_fusion.1
  402.7 2.5 multiply_reduce_fusion.5
  406.8 6.4 %multiply_reduce_fusion = (f32[6,512]{1,0:T(8,128)S(1)}, f32[6,512,1024]{2,1,0:T(8,128)}) fusion(f32[6,512,1024]{2,1,0:T(8,128)S(1)} %bitcast.196, f32[6,512]{1,0:T(8,128)S(1)} %copy-done.48, pred[1024]{0:T(1024)(128)(4,1)S(1)} %add_compare_fusion, bf16[6,512,64]{1,2,0:T(8,128)(2,1)S(1)} %bitcast.256, bf16[6,1024,64]{1,2,0:T(8,128)(2,1)S(1)} %bitcast.261), kind=kOutput, calls=%fused_computation.1 | convolution fusion | flops 418378752 | bytes 26371072 | tf_op jit(solution)/shard_map/hqd,hkd->hqk/dot_general | solution.py:1092
  413.2 3.3 bitcast_reduce_fusion
  416.6 7.1 %multiply_convert_fusion = bf16[6,512,1024]{2,1,0:T(8,128)(2,1)S(1)} fusion(f32[6,512,1024]{2,1,0:T(8,128)} %get-tuple-element.141, f32[6,512,1024]{2,1,0:T(8,128)S(1)} %bitcast.196, f32[6,512]{1,0:T(8,128)S(1)} %get-tuple-element.140, f32[6,512]{1,0:T(8,128)S(1)} %copy-done.48, pred[1024]{0:T(1024)(128)(4,1)S(1)} %add_compare_fusion), kind=kLoop, calls=%fused_computation | loop fusion | flops 18874368 | bytes 31482880 | tf_op jit(solution)/shard_map/convert_element_type | solution.py:1094
  424.9 2.1 bitcast_reduce_fusion.2
  441.9 16.4 %collective-permute-done.12 = bf16[512,768]{1,0:T(8,128)(2,1)S(1)} collective-permute-done((bf16[512,768]{1,0:T(8,128)(2,1)S(1)}, bf16[512,768]{1,0:T(8,128)(2,1)S(1)}, u32[]{:S(2)}, u32[]{:S(2)}) %collective-permute-start.12) | collective-permute-done | bytes 786464 | tf_op jit(solution)/shard_map/ppermute | solution.py:1035
  458.3 2.6 add_convert_fusion.2
  460.9 148.1 %reduce_all.1 = (f32[2,24,1152]{2,1,0:T(8,128)}, f32[2,24,1536]{2,1,0:T(8,128)}, f32[24,768]{1,0:T(8,128)}, f32[96,768]{1,0:T(8,128)}, f32[2,24,1152]{2,1,0:T(8,...) custom-call(bf16[2,2,4,2,24,1152]{5,4,3,2,1,0:T(8,128)(2,1)} %pad_ma, ...), custom_call_target="tpu_custom_call" | custom-call | tf_op jit(solution)/shard_map/reduce_all/pallas_call | solution.py:1021
  (440 shorter events, 106.5 us)
Async XLA Ops:
  0.7 4.9 copy-start.42
  0.7 6.3 %copy-start.85 = (bf16[2,24]{1,0:T(2,128)(2,1)S(1)}, bf16[2,24]{1,0:T(2,128)(2,1)}, u32[]{:S(2)}) copy-start(bf16[2,24]{1,0:T(2,128)(2,1)} %param.29) | copy-start | bytes 292
  0.7 6.3 %copy-start.86 = (bf16[2,24]{1,0:T(2,128)(2,1)S(1)}, bf16[2,24]{1,0:T(2,128)(2,1)}, u32[]{:S(2)}) copy-start(bf16[2,24]{1,0:T(2,128)(2,1)} %param.30) | copy-start | bytes 292
  0.7 6.3 %copy-start.87 = (bf16[2,24]{1,0:T(2,128)(2,1)S(1)}, bf16[2,24]{1,0:T(2,128)(2,1)}, u32[]{:S(2)}) copy-start(bf16[2,24]{1,0:T(2,128)(2,1)} %param.31) | copy-start | bytes 292
  0.7 6.3 %copy-start.93 = (bf16[2,96]{1,0:T(2,128)(2,1)S(1)}, bf16[2,96]{1,0:T(2,128)(2,1)}, u32[]{:S(2)}) copy-start(bf16[2,96]{1,0:T(2,128)(2,1)} %param.32) | copy-start | bytes 1156
  0.7 6.3 %copy-start.88 = (bf16[2,24]{1,0:T(2,128)(2,1)S(1)}, bf16[2,24]{1,0:T(2,128)(2,1)}, u32[]{:S(2)}) copy-start(bf16[2,24]{1,0:T(2,128)(2,1)} %param.33) | copy-start | bytes 292
  0.7 6.3 %copy-start.89 = (bf16[2,24]{1,0:T(2,128)(2,1)S(1)}, bf16[2,24]{1,0:T(2,128)(2,1)}, u32[]{:S(2)}) copy-start(bf16[2,24]{1,0:T(2,128)(2,1)} %param.34) | copy-start | bytes 292
  0.7 6.3 %copy-start.90 = (bf16[2,24]{1,0:T(2,128)(2,1)S(1)}, bf16[2,24]{1,0:T(2,128)(2,1)}, u32[]{:S(2)}) copy-start(bf16[2,24]{1,0:T(2,128)(2,1)} %param.35) | copy-start | bytes 292
  0.7 6.3 %copy-start.91 = (bf16[2,24]{1,0:T(2,128)(2,1)S(1)}, bf16[2,24]{1,0:T(2,128)(2,1)}, u32[]{:S(2)}) copy-start(bf16[2,24]{1,0:T(2,128)(2,1)} %param.36) | copy-start | bytes 292
  0.7 6.3 %copy-start.92 = (bf16[2,24]{1,0:T(2,128)(2,1)S(1)}, bf16[2,24]{1,0:T(2,128)(2,1)}, u32[]{:S(2)}) copy-start(bf16[2,24]{1,0:T(2,128)(2,1)} %param.37) | copy-start | bytes 292
  176.7 42.6 %copy-start.55 = (f32[768]{0:T(1024)}, f32[768]{0:T(1024)S(1)}, u32[]{:S(2)}) copy-start(f32[768]{0:T(1024)S(1)} %get-tuple-element.91) | copy-start | bytes 9220
  176.7 42.6 %copy-start.73 = (f32[768]{0:T(1024)}, f32[768]{0:T(1024)S(1)}, u32[]{:S(2)}) copy-start(f32[768]{0:T(1024)S(1)} %get-tuple-element.90) | copy-start | bytes 9220
  176.7 43.7 %copy-start.59 = (f32[768]{0:T(1024)}, f32[768]{0:T(1024)S(1)}, u32[]{:S(2)}) copy-start(f32[768]{0:T(1024)S(1)} %get-tuple-element.87) | copy-start | bytes 9220
  192.2 7.5 %copy-start.32 = (bf16[1024,384]{0,1:T(8,128)(2,1)}, bf16[1024,384]{0,1:T(8,128)(2,1)S(1)}, u32[]{:S(2)}) copy-start(bf16[1024,384]{0,1:T(8,128)(2,1)S(1)} %add_convert_fusion.7) | copy-start | bytes 2359300
  192.2 7.5 %copy-start.18 = (bf16[2,4,2,24,768]{4,3,2,1,0:T(8,128)(2,1)S(1)}, bf16[2,4,2,24,768]{4,3,2,1,0:T(8,128)(2,1)}, u32[]{:S(2)}) copy-start(bf16[2,4,2,24,768]{4,3,2,1,0:T(8,128)(2,1)} %get-tuple-element.44) | copy-start | bytes 1769476
  200.5 2.3 collective-permute-start
  205.4 14.0 %copy-start.60 = (f32[512]{0:T(512)}, f32[512]{0:T(512)S(1)}, u32[]{:S(2)}) copy-start(f32[512]{0:T(512)S(1)} %broadcast_multiply_fusion.10) | copy-start | bytes 6148
  205.7 13.7 %copy-start.64 = (f32[512]{0:T(512)}, f32[512]{0:T(512)S(1)}, u32[]{:S(2)}) copy-start(f32[512]{0:T(512)S(1)} %add_rsqrt_fusion.3) | copy-start | bytes 6148
  205.7 9.9 %copy-start.96 = (bf16[2,4,2,96,768]{4,3,2,1,0:T(8,128)(2,1)S(1)}, bf16[2,4,2,96,768]{4,3,2,1,0:T(8,128)(2,1)}, u32[]{:S(2)}) copy-start(bf16[2,4,2,96,768]{4,3,2,1,0:T(8,128)(2,1)} %get-tuple-element.46) | copy-start | bytes 7077892
  217.0 2.4 collective-permute-start.1
  221.7 19.9 %collective-permute-start.2 = (bf16[512,768]{1,0:T(8,128)(2,1)}, bf16[512,768]{1,0:T(8,128)(2,1)}, u32[]{:S(2)}, u32[]{:S(2)}) collective-permute-start(bf16[512,768]{1,0:T(8,128)(2,1)} %fusion.21), channel_id=1, source_target_pairs={{0,1},{1,0},{2,3},{3,2},{4,5},{5,4},{6,7},{7,6},{8,9},{9,8},{10,11... | collective-permute-start | bytes 2359304 | tf_op jit(solution)/shard_map/ppermute | solution.py:1035
  245.9 6.7 %copy-start.1 = (f32[6,512,1024]{2,1,0:T(8,128)}, f32[6,512,1024]{2,1,0:T(8,128)S(1)}, u32[]{:S(2)}) copy-start(f32[6,512,1024]{2,1,0:T(8,128)S(1)} %get-tuple-element.136) | copy-start | bytes 37748740
  257.2 4.7 collective-permute-start.3
  264.1 9.9 %copy-start.2 = (f32[512,768]{1,0:T(8,128)}, f32[512,768]{1,0:T(8,128)S(1)}, u32[]{:S(2)}) copy-start(f32[512,768]{1,0:T(8,128)S(1)} %get-tuple-element.111) | copy-start | bytes 4718596
  264.1 9.9 %copy-start.62 = (f32[512]{0:T(512)}, f32[512]{0:T(512)S(1)}, u32[]{:S(2)}) copy-start(f32[512]{0:T(512)S(1)} %broadcast_multiply_fusion.8) | copy-start | bytes 6148
  264.5 9.6 %copy-start.66 = (f32[512]{0:T(512)}, f32[512]{0:T(512)S(1)}, u32[]{:S(2)}) copy-start(f32[512]{0:T(512)S(1)} %add_rsqrt_fusion.1) | copy-start | bytes 6148
  264.5 9.6 %copy-start.100 = (bf16[2,4,2,96,768]{4,3,2,1,0:T(8,128)(2,1)S(1)}, bf16[2,4,2,96,768]{4,3,2,1,0:T(8,128)(2,1)}, u32[]{:S(2)}) copy-start(bf16[2,4,2,96,768]{4,3,2,1,0:T(8,128)(2,1)} %get-tuple-element.51) | copy-start | bytes 7077892
  276.4 19.6 %collective-permute-start.4 = (bf16[512,768]{1,0:T(8,128)(2,1)}, bf16[512,768]{1,0:T(8,128)(2,1)}, u32[]{:S(2)}, u32[]{:S(2)}) collective-permute-start(bf16[512,768]{1,0:T(8,128)(2,1)} %convolution_convert_fusion.10), channel_id=1, source_target_pairs={{0,8},{8,0},{1,9},{9,1},{2,10},{10,2},{3,11},{11,3},{4,12},{12,4},... | collective-permute-start | bytes 2359304 | tf_op jit(solution)/shard_map/ppermute | solution.py:1035
  307.9 22.7 %collective-permute-start.5 = (bf16[512,768]{1,0:T(8,128)(2,1)}, bf16[512,768]{1,0:T(8,128)(2,1)}, u32[]{:S(2)}, u32[]{:S(2)}) collective-permute-start(bf16[512,768]{1,0:T(8,128)(2,1)} %convolution_convert_fusion.9), channel_id=1, source_target_pairs={{0,8},{8,0},{1,9},{9,1},{2,10},{10,2},{3,11},{11,3},{4,12},{12,4},... | collective-permute-start | bytes 2359304 | tf_op jit(solution)/shard_map/ppermute | solution.py:1035
  322.6 4.9 copy-start.76
  322.6 4.9 copy-start.113
  327.5 8.1 %slice-start.3 = ((s8[12582912]{0:T(1024)(128)(4,1)}), s8[4194304]{0:T(1024)(128)(4,1)S(1)}, s32[]{:S(2)}) async-start(s8[12582912]{0:T(1024)(128)(4,1)} %bitcast.197), calls=%async_computation.3 | async-start | bytes 8388608
  327.6 8.1 %slice-start.4 = ((s8[12582912]{0:T(1024)(128)(4,1)}), s8[4194304]{0:T(1024)(128)(4,1)S(1)}, s32[]{:S(2)}) async-start(s8[12582912]{0:T(1024)(128)(4,1)} %bitcast.197), calls=%async_computation.4 | async-start | bytes 8388608
  330.6 5.1 slice-start.5
  357.1 5.1 collective-permute-start.7
  360.4 5.6 collective-permute-start.6
  362.4 19.5 %collective-permute-start.8 = (bf16[512,768]{1,0:T(8,128)(2,1)S(1)}, bf16[512,768]{1,0:T(8,128)(2,1)S(1)}, u32[]{:S(2)}, u32[]{:S(2)}) collective-permute-start(bf16[512,768]{1,0:T(8,128)(2,1)S(1)} %add_convert_fusion.5), channel_id=1, source_target_pairs={{0,1},{1,0},{2,3},{3,2},{4,5},{5,4},{6,7},{7,6},{8,9},{9,8},{10,11... | collective-permute-start | bytes 2359304 | tf_op jit(solution)/shard_map/ppermute | solution.py:1035
  383.4 5.1 copy-start.8
  392.2 10.4 %collective-permute-start.9 = (bf16[512,768]{1,0:T(8,128)(2,1)}, bf16[512,768]{1,0:T(8,128)(2,1)}, u32[]{:S(2)}, u32[]{:S(2)}) collective-permute-start(bf16[512,768]{1,0:T(8,128)(2,1)} %convolution_convert_fusion.7), channel_id=1, source_target_pairs={{0,8},{8,0},{1,9},{9,1},{2,10},{10,2},{3,11},{11,3},{4,12},{12,4},... | collective-permute-start | bytes 2359304 | tf_op jit(solution)/shard_map/ppermute | solution.py:1035
  399.6 7.1 %slice-start = ((s8[12582912]{0:T(1024)(128)(4,1)}), s8[4194304]{0:T(1024)(128)(4,1)S(1)}, s32[]{:S(2)}) async-start(s8[12582912]{0:T(1024)(128)(4,1)} %bitcast.195), calls=%async_computation | async-start | bytes 8388608
  399.6 7.1 %slice-start.1 = ((s8[12582912]{0:T(1024)(128)(4,1)}), s8[4194304]{0:T(1024)(128)(4,1)S(1)}, s32[]{:S(2)}) async-start(s8[12582912]{0:T(1024)(128)(4,1)} %bitcast.195), calls=%async_computation.1 | async-start | bytes 8388608
  416.5 11.5 %copy-start.36 = (bf16[6,64,1024]{2,1,0:T(8,128)(2,1)}, bf16[6,64,1024]{2,1,0:T(8,128)(2,1)S(1)}, u32[]{:S(2)}) copy-start(bf16[6,64,1024]{2,1,0:T(8,128)(2,1)S(1)} %get-tuple-element.145) | copy-start | bytes 2359300
  416.5 7.1 %copy-start.23 = (bf16[512,384]{0,1:T(8,128)(2,1)S(1)}, bf16[512,384]{0,1:T(8,128)(2,1)}, u32[]{:S(2)}) copy-start(bf16[512,384]{0,1:T(8,128)(2,1)} %copy-done.22) | copy-start | bytes 1179652
  430.2 6.2 %collective-permute-start.11 = (bf16[512,768]{1,0:T(8,128)(2,1)}, bf16[512,768]{1,0:T(8,128)(2,1)}, u32[]{:S(2)}, u32[]{:S(2)}) collective-permute-start(bf16[512,768]{1,0:T(8,128)(2,1)} %slice.277), channel_id=1, source_target_pairs={{0,8},{8,0},{1,9},{9,1},{2,10},{10,2},{3,11},{11,3},{4,12},{12,4},... | collective-permute-start | bytes 2359304 | tf_op jit(solution)/shard_map/ppermute | solution.py:1035
  432.1 9.7 %collective-permute-start.10 = (bf16[512,768]{1,0:T(8,128)(2,1)}, bf16[512,768]{1,0:T(8,128)(2,1)}, u32[]{:S(2)}, u32[]{:S(2)}) collective-permute-start(bf16[512,768]{1,0:T(8,128)(2,1)} %fusion.16), channel_id=1, source_target_pairs={{0,8},{8,0},{1,9},{9,1},{2,10},{10,2},{3,11},{11,3},{4,12},{12,4},... | collective-permute-start | bytes 2359304 | tf_op jit(solution)/shard_map/ppermute | solution.py:1035
  438.3 20.0 %collective-permute-start.12 = (bf16[512,768]{1,0:T(8,128)(2,1)S(1)}, bf16[512,768]{1,0:T(8,128)(2,1)S(1)}, u32[]{:S(2)}, u32[]{:S(2)}) collective-permute-start(bf16[512,768]{1,0:T(8,128)(2,1)S(1)} %add_convert_fusion.3), channel_id=1, source_target_pairs={{0,1},{1,0},{2,3},{3,2},{4,5},{5,4},{6,7},{7,6},{8,9},{9,8},{10,11... | collective-permute-start | bytes 2359304 | tf_op jit(solution)/shard_map/ppermute | solution.py:1035
  616.5 5.0 copy-start.43
  616.5 5.0 copy-start.44
  (85 other events, 246.7 us)
